TPU v7x, 32 devices: a whole 2x2x4 slice. The times are simulated.
32 devices in a mesh: dp: 8 (over y, x, core), tensor: 4 (over z).
Axes of the slice: x: 2, y: 2, z: 4, core: 2. Of those that a mesh axis runs over, the one named last changes fastest.
Arguments:
- tokens: bfloat16 [4096, 2048], P('dp'), may hold values from -6 to 6
- segment_ids: int32 [8, 512], P('dp'), may hold values from 0 to 15, never falling along the last dimension, each value on 1 to 256 neighbouring positions
- norm_gain: bfloat16 [2048], replicated, may hold values from 0.099609375 to 1.8984375
- norm_bias: bfloat16 [2048], replicated, may hold values from -2 to 2
- qkv_weight: bfloat16 [2048, 6144], P(None, 'tensor'), may hold values from -0.125 to 0.125
- qkv_bias: bfloat16 [6144], P('tensor'), may hold values from -2 to 2
- out_weight: bfloat16 [2048, 2048], P('tensor'), may hold values from -0.5 to 0.5
- gate_weight: bfloat16 [2048, 5632], P(None, 'tensor'), may hold values from -0.125 to 0.125
- up_weight: bfloat16 [2048, 5632], P(None, 'tensor'), may hold values from -0.125 to 0.125
- down_weight: bfloat16 [5632, 2048], P('tensor'), may hold values from -0.078125 to 0.078125
- cotangent: bfloat16 [4096, 2048], P('dp'), may hold values from -6 to 6
Outputs:
- output: bfloat16 [4096, 2048], P('dp')
- grad_input: bfloat16 [4096, 2048], P('dp')
- grad_gain: float32 [2048], replicated
- grad_norm_bias: float32 [2048], replicated
- grad_qkv_weight: float32 [2048, 6144], P('dp', 'tensor')
- grad_qkv_bias: float32 [6144], P('tensor')
- grad_out_weight: float32 [2048, 2048], P('tensor', 'dp')
- grad_gate_weight: float32 [2048, 5632], P('dp', 'tensor')
- grad_up_weight: float32 [2048, 5632], P('dp', 'tensor')
- grad_down_weight: float32 [5632, 2048], P('tensor', 'dp')
Inputs may be any that keep to these rules, and one draw needn't show every extreme that they name: `segment_ids`: ids never fall along a sequence; each document has 1 to 256 tokens, and every sequence has one document of exactly 256 tokens.
All inputs are finite; a program needn't handle non-finite values.
Results may differ from a plain program's by a relative error of at most 0.0096.
Values may be sent and summed in bfloat16 or wider, within the bound.
A program may use at most 256 MiB of HBM per device.

v0:
```python
import functools

import jax
import jax.numpy as jnp
from jax import lax
from jax.experimental import pallas as pl
from jax.experimental.pallas import tpu as pltpu
from jax.sharding import PartitionSpec as P

DH = 64
ROT = 16


EPSILON = 1e-05
NEGATIVE = -1e30


def positions_of(segments):
    column = jnp.arange(segments.shape[1], dtype=jnp.int32)
    starts = jnp.concatenate(
        [jnp.ones((segments.shape[0], 1), dtype=bool), segments[:, 1:] != segments[:, :-1]], axis=1
    )
    doc_start = lax.cummax(jnp.where(starts, column[None, :], 0), axis=1)
    return column[None, :] - doc_start


def rotary_tables(positions):
    half_rot = ROT // 2
    frequency = jnp.power(10000.0, -2.0 * jnp.arange(half_rot, dtype=jnp.float32) / ROT)
    angles = positions.astype(jnp.float32)[:, None] * frequency[None, :]
    return (jnp.cos(angles)[:, None, :], jnp.sin(angles)[:, None, :])


def rotate(tensor, cosine, sine_table):
    half_rot = ROT // 2
    first_half = tensor[..., :half_rot]
    second_half = tensor[..., half_rot:ROT]
    return jnp.concatenate(
        [
            first_half * cosine - second_half * sine_table,
            second_half * cosine + first_half * sine_table,
            tensor[..., ROT:],
        ],
        axis=-1,
    )


def rotate_back(tensor, cosine, sine_table):
    half_rot = ROT // 2
    first_half = tensor[..., :half_rot]
    second_half = tensor[..., half_rot:ROT]
    return jnp.concatenate(
        [
            first_half * cosine + second_half * sine_table,
            second_half * cosine - first_half * sine_table,
            tensor[..., ROT:],
        ],
        axis=-1,
    )


def masked_scores(query_block, seq_keys, seq_segments, begin_row, block_rows):
    key_index = jnp.arange(seq_keys.shape[0], dtype=jnp.int32)
    allowed = (seq_segments[begin_row : begin_row + block_rows, None] == seq_segments[None, :]) & (
        key_index[:, None] >= key_index[None, :]
    )
    scores = jnp.einsum("qhd,khd->hqk", query_block, seq_keys, preferred_element_type=jnp.float32)
    return jnp.where(allowed[None], scores, NEGATIVE)


def attend_forward(packed):
    seq_queries, seq_keys, seq_values, seq_segments = packed
    length = seq_queries.shape[0]
    block_rows = min(512, length)
    scores = masked_scores(seq_queries, seq_keys, seq_segments, 0, block_rows)
    top_score = jnp.max(scores, -1, keepdims=True)
    weights = jnp.exp(scores - top_score)
    denominator = jnp.sum(weights, -1, keepdims=True)
    probability = (weights / denominator).astype(jnp.bfloat16)
    contexts = [
        jnp.einsum("hqk,khd->qhd", probability, seq_values, preferred_element_type=jnp.float32)
    ]
    log_totals = [top_score + jnp.log(denominator)]
    return (jnp.concatenate(contexts, 0), jnp.concatenate(log_totals, 1))


def attend_backward(packed):
    seq_queries, seq_keys, seq_values, seq_segments, seq_log_total, seq_grad_context = packed
    length = seq_queries.shape[0]
    block_rows = min(512, length)
    grad_keys = jnp.zeros(seq_keys.shape, jnp.float32)
    grad_values = jnp.zeros(seq_values.shape, jnp.float32)
    scores = masked_scores(seq_queries, seq_keys, seq_segments, 0, block_rows)
    probability = jnp.exp(scores - seq_log_total[:, 0:block_rows])
    grad_prob = jnp.einsum(
        "qhd,khd->hqk", seq_grad_context, seq_values, preferred_element_type=jnp.float32
    )
    row_dot = jnp.sum(probability * grad_prob, -1, keepdims=True)
    grad_scores = (probability * (grad_prob - row_dot)).astype(jnp.bfloat16)
    grad_queries = [
        jnp.einsum("hqk,khd->qhd", grad_scores, seq_keys, preferred_element_type=jnp.float32)
    ]
    grad_keys = grad_keys + jnp.einsum(
        "hqk,qhd->khd", grad_scores, seq_queries, preferred_element_type=jnp.float32
    )
    grad_values = grad_values + jnp.einsum(
        "hqk,qhd->khd",
        probability.astype(jnp.bfloat16),
        seq_grad_context,
        preferred_element_type=jnp.float32,
    )
    return (jnp.concatenate(grad_queries, 0), grad_keys, grad_values)


def contract_rows(left_side, right_side):
    return lax.dot_general(
        left_side, right_side, (((0,), (0,)), ((), ())), preferred_element_type=jnp.float32
    )


def contract_cols(left_side, right_side):
    return lax.dot_general(
        left_side, right_side, (((1,), (1,)), ((), ())), preferred_element_type=jnp.float32
    )


def norm_back(grad_normed_out, normed, inverse_std, gain_full):
    grad_normed = grad_normed_out * gain_full
    return inverse_std * (
        grad_normed
        - jnp.mean(grad_normed, -1, keepdims=True)
        - normed * jnp.mean(grad_normed * normed, -1, keepdims=True)
    )


def local(
    tokens,
    segment_ids,
    norm_gain,
    norm_bias,
    qkv_weight,
    qkv_bias,
    out_weight,
    gate_weight,
    up_weight,
    down_weight,
    cotangent,
):
    row_count = tokens.shape[0]
    seq_count, length = segment_ids.shape
    head_count = qkv_weight.shape[1] // (3 * DH)
    score_scale = DH ** (-0.5)
    inputs = tokens.astype(jnp.float32)
    row_mean = jnp.mean(inputs, -1, keepdims=True)
    centered = inputs - row_mean
    inverse_std = lax.rsqrt(jnp.mean(centered * centered, -1, keepdims=True) + EPSILON)
    normed = centered * inverse_std
    gain_full = norm_gain.astype(jnp.float32)
    hidden_in = (normed * gain_full + norm_bias.astype(jnp.float32)).astype(jnp.bfloat16)
    joined_qkv = (
        jnp.dot(hidden_in, qkv_weight, preferred_element_type=jnp.float32)
        + qkv_bias.astype(jnp.float32)
    ).reshape(row_count, head_count, 3, DH)
    positions = positions_of(segment_ids).reshape(row_count)
    cosine, sine_table = rotary_tables(positions)
    queries = (rotate(joined_qkv[:, :, 0], cosine, sine_table) * score_scale).astype(jnp.bfloat16)
    key_rows = rotate(joined_qkv[:, :, 1], cosine, sine_table).astype(jnp.bfloat16)
    value_rows = joined_qkv[:, :, 2].astype(jnp.bfloat16)
    seq_shape = (seq_count, length, head_count, DH)
    seq_queries = queries.reshape(seq_shape)
    seq_keys = key_rows.reshape(seq_shape)
    seq_values = value_rows.reshape(seq_shape)
    context, log_total = lax.map(attend_forward, (seq_queries, seq_keys, seq_values, segment_ids))
    context = context.reshape(row_count, head_count * DH).astype(jnp.bfloat16)
    gate_pre = jnp.dot(hidden_in, gate_weight, preferred_element_type=jnp.float32)
    up_pre = jnp.dot(hidden_in, up_weight, preferred_element_type=jnp.float32)
    sigmoid_gate = jax.nn.sigmoid(gate_pre)
    activated = gate_pre * sigmoid_gate
    mixed = (activated * up_pre).astype(jnp.bfloat16)
    partial_out = jnp.dot(context, out_weight, preferred_element_type=jnp.float32) + jnp.dot(
        mixed, down_weight, preferred_element_type=jnp.float32
    )
    summed = lax.psum(partial_out, "tensor")
    output = (inputs + summed).astype(jnp.bfloat16)
    grad_context = contract_cols(cotangent, out_weight).astype(jnp.bfloat16)
    grad_out_w = contract_rows(context, cotangent)
    grad_down_w = contract_rows(mixed, cotangent)
    grad_out_part, grad_down_part = (
        lax.psum_scatter(grad_out_w, "dp", scatter_dimension=1, tiled=True),
        lax.psum_scatter(grad_down_w, "dp", scatter_dimension=1, tiled=True),
    )
    grad_mixed = contract_cols(cotangent, down_weight)
    grad_up = (grad_mixed * activated).astype(jnp.bfloat16)
    grad_gate = (
        grad_mixed * up_pre * sigmoid_gate * (1.0 + gate_pre * (1.0 - sigmoid_gate))
    ).astype(jnp.bfloat16)
    grad_gate_w = contract_rows(hidden_in, grad_gate)
    grad_up_w = contract_rows(hidden_in, grad_up)
    grad_hidden = contract_cols(grad_gate, gate_weight) + contract_cols(grad_up, up_weight)
    grad_queries, grad_keys, grad_values = lax.map(
        attend_backward,
        (
            seq_queries,
            seq_keys,
            seq_values,
            segment_ids,
            log_total,
            grad_context.reshape(seq_shape),
        ),
    )
    flat_shape = (row_count, head_count, DH)
    grad_queries = rotate_back(grad_queries.reshape(flat_shape) * score_scale, cosine, sine_table)
    grad_keys = rotate_back(grad_keys.reshape(flat_shape), cosine, sine_table)
    grad_joined = (
        jnp.stack([grad_queries, grad_keys, grad_values.reshape(flat_shape)], axis=2)
        .reshape(row_count, head_count * 3 * DH)
        .astype(jnp.bfloat16)
    )
    bias_local = jnp.sum(grad_joined.astype(jnp.float32), 0)
    grad_qkv_w = contract_rows(hidden_in, grad_joined)
    grad_hidden = grad_hidden + contract_cols(grad_joined, qkv_weight)
    grad_qkv_part, grad_gate_part, grad_up_part = (
        lax.psum_scatter(grad_qkv_w, "dp", scatter_dimension=0, tiled=True),
        lax.psum_scatter(grad_gate_w, "dp", scatter_dimension=0, tiled=True),
        lax.psum_scatter(grad_up_w, "dp", scatter_dimension=0, tiled=True),
    )
    grad_total = lax.psum(grad_hidden, "tensor")
    grad_input = (
        cotangent.astype(jnp.float32) + norm_back(grad_total, normed, inverse_std, gain_full)
    ).astype(jnp.bfloat16)
    grad_gain, grad_shift, grad_bias = lax.psum(
        (jnp.sum(grad_total * normed, 0), jnp.sum(grad_total, 0), bias_local), "dp"
    )
    return (
        output,
        grad_input,
        grad_gain,
        grad_shift,
        grad_qkv_part,
        grad_bias,
        grad_out_part,
        grad_gate_part,
        grad_up_part,
        grad_down_part,
    )


BF = jnp.bfloat16
F32 = jnp.float32
MESH = pl.DeviceIdType.MESH
W = 256
PR = 32
SMALL_AT = 2


def comm_kernel(
    dims,
    hid_h, cot_h, tok_h, ctx_h, gj_h, gain_ref, bias_ref, qkv_h, out_h, gate_h, up_h, down_h,
    out_o, gin_o, sv_o, sums_o,
    hid_t, cot, cot_s, tok, ctx, gj, w_a, w_b, w_d, acc, gu, s1, own, recv1, recv2, recv3,
    zs, ze, zm, stage, svb, svr, svq,
    ld_sem, w_sem, s1_send, s1_recv, s2_send, s2_recv, s3_send, s3_recv,
    e_send, e_recv, m_send, m_recv, o_send, o_recv, o_loc, st_sem, v_send, v_recv,
):
    rows, width, full, tail, n_out, n_qkv, n_batch = dims
    n_piece = rows // PR
    hid = zs.at[1]
    dp = lax.axis_index("dp")
    zi = lax.axis_index("tensor")
    c = lax.rem(dp, 2)
    x = lax.rem(dp // 2, 2)
    y = dp // 4
    core_dev = {"dp": dp + 1 - 2 * c}
    x_dev = {"dp": dp + 2 - 4 * x}
    y_dev = {"dp": dp + 4 - 8 * y}
    is_mid = (zi == 1) | (zi == 2)
    is_end = (zi == 0) | (zi == 3)
    end_of = jnp.where(zi == 1, 0, 3)
    mid_of_end = jnp.where(zi == 0, 1, 2)
    end_dev = {"tensor": end_of}
    mid_dev = {"tensor": mid_of_end}
    other_mid = {"tensor": 3 - zi}

    def load(src, dst, k):
        return pltpu.make_async_copy(src, dst, ld_sem.at[k])

    def w_out(j):
        return pltpu.make_async_copy(out_h.at[pl.ds(j * W, W), :], w_d, w_sem.at[2])

    def w_down(i):
        return pltpu.make_async_copy(down_h.at[pl.ds(i * W, W), :], w_d, w_sem.at[2])

    def w_gate(i):
        return pltpu.make_async_copy(gate_h.at[:, pl.ds(i * W, W)], w_a, w_sem.at[0])

    def w_up(i):
        return pltpu.make_async_copy(up_h.at[:, pl.ds(i * W, W)], w_b, w_sem.at[1])

    def w_qkv(j):
        return pltpu.make_async_copy(qkv_h.at[:, pl.ds(j * W, W)], w_a, w_sem.at[0])

    t0 = full * W
    w_gate_t = pltpu.make_async_copy(gate_h.at[:, pl.ds(t0, tail)], w_a.at[:, 0:tail], w_sem.at[0])
    w_up_t = pltpu.make_async_copy(up_h.at[:, pl.ds(t0, tail)], w_a.at[:, tail : 2 * tail], w_sem.at[1])
    w_down_t = pltpu.make_async_copy(down_h.at[pl.ds(t0, tail), :], w_d.at[0:tail, :], w_sem.at[2])

    ctx_ld = load(ctx_h, ctx, 0)
    hid_ld = load(hid_h, hid, 1)
    cot_ld = load(cot_h, cot, 2)
    gj_ld = load(gj_h, gj, 3)
    tok_ld = load(tok_h, tok, 4)
    cs_ld = [
        load(cot_h.at[:, (2 * q + s) * W : (2 * q + s + 1) * W], cot_s.at[s, :, q * W : (q + 1) * W], 5 + 2 * q + s)
        for q in range(4)
        for s in range(2)
    ]
    ctx_ld.start()
    w_out(0).start()
    for cp in cs_ld:
        cp.start()
    hid_ld.start()
    w_gate(0).start()
    w_up(0).start()
    cot_ld.start()
    gj_ld.start()
    tok_ld.start()

    barrier = pltpu.get_barrier_semaphore()
    for dev in (core_dev, x_dev, y_dev, {"dp": dp + 2 - 4 * x + 4 - 8 * y}):
        pl.semaphore_signal(barrier, inc=1, device_id=dev, device_id_type=MESH)

    @pl.when(is_mid)
    def _():
        pl.semaphore_signal(barrier, inc=1, device_id=end_dev, device_id_type=MESH)
        pl.semaphore_signal(barrier, inc=1, device_id=other_mid, device_id_type=MESH)

    @pl.when(is_end)
    def _():
        pl.semaphore_signal(barrier, inc=1, device_id=mid_dev, device_id_type=MESH)

    pl.semaphore_wait(barrier, jnp.where(is_mid, 6, 5))

    def rdma(src, dst, send, recv, dev):
        return pltpu.make_async_remote_copy(
            src_ref=src, dst_ref=dst, send_sem=send, recv_sem=recv, device_id=dev, device_id_type=MESH
        )

    def c1(b):
        slot = lax.rem(b, 4)
        return rdma(s1.at[slot], recv1.at[b], s1_send.at[slot], s1_recv.at[b], core_dev)

    def c2(b, h):
        if h == 0:
            return rdma(recv1.at[b, :, 1 - x, 0], recv2.at[b, 0], s2_send.at[b, 0], s2_recv.at[b, 0], x_dev)
        return rdma(recv1.at[b, 1 - y, :, 1], recv2.at[b, 1], s2_send.at[b, 1], s2_recv.at[b, 1], y_dev)

    def c3(b, h):
        if h == 0:
            return rdma(recv2.at[b, 0, 1 - y], recv3.at[b, 0], s3_send.at[b, 0], s3_recv.at[b, 0], y_dev)
        return rdma(recv2.at[b, 1, 1 - x], recv3.at[b, 1], s3_send.at[b, 1], s3_recv.at[b, 1], x_dev)

    def up32(v):
        return v.astype(F32)

    def ev1(b):
        slot = lax.rem(b, 4)
        c1(b).wait_recv()
        for yy in range(2):
            for xx in range(2):
                for h in range(2):
                    recv1[b, yy, xx, h] += own[slot, yy, xx, h]
        c2(b, 0).start()
        c2(b, 1).start()

    def ev2(b):
        c2(b, 0).wait_recv()
        c2(b, 1).wait_recv()
        for k in range(2):
            recv2[b, 0, k] += recv1[b, k, x, 0]
            recv2[b, 1, k] += recv1[b, y, k, 1]
        c3(b, 0).start()
        c3(b, 1).start()

    def st_copy(b):
        slot = lax.rem(b, 2)
        return pltpu.make_async_copy(stage.at[slot], sums_o.at[b], st_sem.at[slot])

    def ev3(b):
        slot = lax.rem(b, 2)
        c3(b, 0).wait_recv()
        c3(b, 1).wait_recv()

        @pl.when(b >= 2)
        def _():
            st_copy(b - 2).wait()

        stage[slot, 0] = up32(recv2[b, 0, y]) + up32(recv3[b, 0])
        stage[slot, 1] = up32(recv2[b, 1, x]) + up32(recv3[b, 1])
        st_copy(b).start()

    def before_put(b):
        @pl.when(b >= 4)
        def _():
            c1(b - 4).wait_send()

    def after_put(b):
        c1(b).start()

        @pl.when(b >= 2)
        def _():
            ev1(b - 2)

    def put_rows(b, grad):
        slot = lax.rem(b, 4)
        before_put(b)
        for part, dst in ((1 - c, s1), (c, own)):
            left = hid_t[:, part].reshape(4 * W, rows)
            res = jnp.dot(left, grad, preferred_element_type=F32).astype(BF)
            dst[slot] = res.reshape(2, 2, 2, W // 2, W)
        after_put(b)

    def put_cols(b, left_t):
        slot = lax.rem(b, 4)
        h = left_t.shape[0]
        before_put(b)
        for part, dst in ((1 - c, s1), (c, own)):
            res = jnp.dot(left_t, cot_s[part], preferred_element_type=F32).astype(BF)
            for q in range(4):
                piece = res[:, q * W : (q + 1) * W].reshape(2, h // 2, W)
                dst[slot, q // 2, q % 2, :, 0 : h // 2, :] = piece
                if h < W:
                    dst[slot, q // 2, q % 2, :, h // 2 :, :] = jnp.zeros((2, (W - h) // 2, W), BF)
        after_put(b)

    NB = 512

    def acc_cols(left, w_ref, k, first):
        for n in range(width // NB):
            cols = slice(n * NB, (n + 1) * NB)
            res = jnp.dot(left, w_ref[0:k, cols], preferred_element_type=F32)
            if first:
                acc[:, cols] = res
            else:
                acc[:, cols] += res

    def acc_rows(grad, w_ref):
        for n in range(width // NB):
            cols = slice(n * NB, (n + 1) * NB)
            acc[:, cols] += lax.dot_general(
                grad, w_ref[cols, :], (((1,), (1,)), ((), ())), preferred_element_type=F32
            )

    def z_rows(p):
        return pl.ds(pl.multiple_of(p * PR, PR), PR)

    def ce(a, p):
        i = a * n_piece + p
        return rdma(zs.at[a, z_rows(p)], ze.at[a, z_rows(p)], e_send.at[i], e_recv.at[i], mid_dev)

    def cm(a, p):
        i = a * n_piece + p
        return rdma(zs.at[a, z_rows(p)], zm.at[a, z_rows(p)], m_send.at[i], m_recv.at[i], other_mid)

    def co(a, p, ref):
        i = a * n_piece + p
        return rdma(ze.at[a, z_rows(p)], ref.at[z_rows(p)], o_send.at[i], o_recv.at[i], end_dev)

    def cl(a, p, ref):
        i = a * n_piece + p
        return pltpu.make_async_copy(ze.at[a, z_rows(p)], ref.at[z_rows(p)], o_loc.at[i])

    def ev_e(e):
        a, p = e // n_piece, lax.rem(e, n_piece)

        @pl.when(is_mid)
        def _():
            ce(a, p).wait_recv()
            r = z_rows(p)
            zs[a, r, :] += ze[a, r, :]
            cm(a, p).start()

    def norm_rows(r):
        v = up32(tok[r, :])
        mu = jnp.mean(v, -1, keepdims=True)
        v = v - mu
        inv = lax.rsqrt(jnp.mean(v * v, -1, keepdims=True) + EPSILON)
        return v * inv, inv

    def ev_m(e):
        a, p = e // n_piece, lax.rem(e, n_piece)

        @pl.when(is_mid)
        def _():
            cm(a, p).wait_recv()
            r = z_rows(p)

            @pl.when(a == 0)
            def _():
                total = up32(zs[0, r, :]) + up32(zm[0, r, :])
                ze[0, r, :] = (up32(tok[r, :]) + total).astype(BF)
                co(0, p, out_o).start()
                cl(0, p, out_o).start()

            @pl.when(a == 1)
            def _():
                total = up32(zs[1, r, :]) + up32(zm[1, r, :])
                normed, inv = norm_rows(r)
                back = norm_back(total, normed, inv, gain_ref[...].astype(F32))
                ze[1, r, :] = (up32(cot[r, :]) + back).astype(BF)
                co(1, p, gin_o).start()
                cl(1, p, gin_o).start()

    ctx_ld.wait()
    for cp in cs_ld:
        cp.wait()
    for j in range(n_out):
        left = ctx[:, j * W : (j + 1) * W]
        w_out(j).wait()
        acc_cols(left, w_d, W, j == 0)
        if j + 1 < n_out:
            w_out(j + 1).start()
        else:
            w_down(0).start()
        put_cols(jnp.int32(j), left.T)
    hid_ld.wait()
    for q in range(4):
        for s in range(2):
            lo = (2 * q + s) * W
            hid_t[q, s] = hid[:, lo : lo + W].T

    def act_of(g, u):
        return (g * jax.nn.sigmoid(g) * u).astype(BF)

    def fwd(i, keep):
        w_gate(i).wait()
        g = jnp.dot(hid[...], w_a[...], preferred_element_type=F32)
        w_up(i).wait()
        u = jnp.dot(hid[...], w_b[...], preferred_element_type=F32)

        @pl.when(i + 1 < full)
        def _():
            w_gate(i + 1).start()
            w_up(i + 1).start()

        @pl.when(i + 1 == full)
        def _():
            w_gate_t.start()
            w_up_t.start()

        gu[i, 0] = g.astype(BF)
        gu[i, 1] = u.astype(BF)
        mixed = act_of(g, u)
        w_down(i).wait()
        acc_cols(mixed, w_d, W, False)

        @pl.when(i + 1 < full)
        def _():
            w_down(i + 1).start()

        @pl.when(i + 1 == full)
        def _():
            w_down_t.start()

        put_cols(n_out + i, mixed.T)
        return keep

    lax.fori_loop(0, full, fwd, 0)
    w_gate_t.wait()
    w_up_t.wait()
    both = jnp.dot(hid[...], w_a[...], preferred_element_type=F32)
    gj_ld.wait()
    w_qkv(0).start()
    gu[full, 0] = both.astype(BF)
    mixed = act_of(both[:, 0:tail], both[:, tail:])
    w_down_t.wait()
    acc_cols(mixed, w_d, tail, False)
    w_down(0).start()
    b0 = n_out + full

    tok_ld.wait()
    cot_ld.wait()

    def cv(k, dev):
        return rdma(svb.at[k], svr.at[k], v_send.at[k], v_recv.at[k], dev)

    def cw(k, dev):
        return rdma(svb.at[4], svq.at[y, x], v_send.at[4 + k], v_recv.at[4 + k], dev)

    square = (x_dev, y_dev, {"dp": dp + 2 - 4 * x + 4 - 8 * y})

    def small_1():
        @pl.when(is_mid)
        def _():
            cv(0, end_dev).wait_recv()
            svb[1] = svb[0] + svr[0]
            cv(1, other_mid).start()

    def small_2():
        @pl.when(is_mid)
        def _():
            cv(1, other_mid).wait_recv()
            svb[2] = svb[1] + svr[1]
            svb[3, 0:2, :] = svb[2, 0:2, :]
            cv(2, end_dev).start()

    def small_3():
        @pl.when(is_end)
        def _():
            cv(2, mid_dev).wait_recv()
            svb[3, 0:2, :] = svr[2, 0:2, :]

        svb[3, 2:8, :] = svb[0, 2:8, :]
        cv(3, core_dev).start()

    def small_4():
        cv(3, core_dev).wait_recv()
        svb[4] = svb[3] + svr[3]
        svq[y, x] = svb[4]
        for k, dev in enumerate(square):
            cw(k, dev).start()

    def small_5():
        for k, dev in enumerate(square):
            cw(k, dev).wait_recv()
        sv_o[...] = (svq[0, 0] + svq[0, 1]) + (svq[1, 0] + svq[1, 1])

    def small_sent():
        @pl.when(is_end)
        def _():
            cv(0, mid_dev).wait_send()

        @pl.when(is_mid)
        def _():
            cv(1, other_mid).wait_send()
            cv(2, end_dev).wait_send()

        cv(3, core_dev).wait_send()
        for k, dev in enumerate(square):
            cw(k, dev).wait_send()

    def to_line(a):
        def step(p, keep):
            r = z_rows(p)
            v = acc[r, :]
            zs[a, r, :] = v.astype(BF)
            if a == 0:
                acc[r, :] = jnp.zeros_like(v)
            else:
                normed, _inv = norm_rows(r)
                svb[0, 0:1, :] += jnp.sum(v * normed, 0, keepdims=True)
                svb[0, 1:2, :] += jnp.sum(v, 0, keepdims=True)

            return keep

        def send(p, keep):
            ce(a, p).start()
            return keep

        lax.fori_loop(0, n_piece, step, 0)

        @pl.when(is_end)
        def _():
            if a == 1:
                cv(0, mid_dev).start()
            lax.fori_loop(0, n_piece, send, 0)

    to_line(0)
    put_cols(jnp.int32(b0), mixed.T)
    b0 = b0 + 1

    def joined(j, keep):
        grad = jnp.concatenate([gj[2 * j], gj[2 * j + 1]], axis=1)
        w_qkv(j).wait()
        acc_rows(grad, w_a)

        @pl.when(j + 1 < n_qkv)
        def _():
            w_qkv(j + 1).start()

        @pl.when(j + 1 == n_qkv)
        def _():
            w_gate(0).start()
            w_up(0).start()

        put_rows(b0 + j, grad)

        @pl.when((j >= 3) & (lax.rem(j, 2) == 1))
        def _():
            ev_e((j - 3) // 2)

        return keep

    lax.fori_loop(0, n_qkv, joined, 0)
    b1 = b0 + n_qkv

    def gate_grads(gm, g, u):
        sg = jax.nn.sigmoid(g)
        g_up = (gm * (g * sg)).astype(BF)
        g_gate = (gm * u * sg * (1.0 + g * (1.0 - sg))).astype(BF)
        return g_gate, g_up

    def cols_t(left, w_ref, k):
        return lax.dot_general(left, w_ref[0:k, :], (((1,), (1,)), ((), ())), preferred_element_type=F32)

    e0 = (n_qkv - 2) // 2

    def bwd(i, keep):
        w_down(i).wait()
        gm = cols_t(cot[...], w_d, W)

        @pl.when(i + 1 < full)
        def _():
            w_down(i + 1).start()

        @pl.when(i + 1 == full)
        def _():
            w_down_t.start()

        g_gate, g_up = gate_grads(gm, up32(gu[i, 0]), up32(gu[i, 1]))
        w_gate(i).wait()
        acc_rows(g_gate, w_a)
        w_up(i).wait()
        acc_rows(g_up, w_b)

        @pl.when(i + 1 < full)
        def _():
            w_gate(i + 1).start()
            w_up(i + 1).start()

        @pl.when(i + 1 == full)
        def _():
            w_gate_t.start()
            w_up_t.start()

        for half, grad in enumerate((g_gate, g_up)):
            put_rows(b1 + 2 * i + half, grad)
            ev_e(e0 + 2 * i + half)
            ev2(2 * i + half)
            ev_m(e0 - 2 + 2 * i + half)
        return keep

    lax.fori_loop(0, full, bwd, 0)
    w_down_t.wait()
    gm = cols_t(cot[...], w_d, tail)
    both = up32(gu[full, 0])
    g_gate, g_up = gate_grads(gm, both[:, 0:tail], both[:, tail:])
    both = jnp.concatenate([g_gate, g_up], axis=1)
    w_gate_t.wait()
    w_up_t.wait()
    acc_rows(both, w_a)
    svb[0] = jnp.zeros_like(svb[0])
    svb[0, 2:3, 0 : n_qkv * W] = bias_ref[...]
    to_line(1)
    b2 = b1 + 2 * full
    e0 = e0 + 2 * full
    put_rows(jnp.int32(b2), both)
    ev_e(jnp.int32(e0))
    ev_m(jnp.int32(e0 - 2))
    ev1(jnp.int32(b2 - 1))
    ev1(jnp.int32(b2))

    n_e = 2 * n_piece
    e0 = e0 + 1
    two = 2 * full
    late = 7
    smalls = (small_1, small_2, small_3, small_4)

    def drain(k, keep):
        @pl.when(k + two < n_batch)
        def _():
            ev2(k + two)

        @pl.when(k + e0 < n_e)
        def _():
            ev_e(k + e0)

        @pl.when(k + e0 - 2 < n_e)
        def _():
            ev_m(k + e0 - 2)

        for i, small in enumerate(smalls):
            pl.when(k == SMALL_AT + i)(small)

        for h in range(2):
            b = 2 * (k - late) + h

            @pl.when((b >= 0) & (b < n_batch))
            def _():
                ev3(b)

        return keep

    lax.fori_loop(0, max(late + (n_batch + 1) // 2, n_e - e0 + 2), drain, 0)
    small_5()

    small_sent()

    def finish(b, keep):
        for h in range(2):
            c2(b, h).wait_send()
            c3(b, h).wait_send()
        return keep

    lax.fori_loop(0, n_batch, finish, 0)
    for k in range(4):
        c1(jnp.int32(n_batch - 4 + k)).wait_send()
    for k in range(2):
        st_copy(jnp.int32(n_batch - 2 + k)).wait()

    def finish_line(p, keep):
        for a, ref in ((0, out_o), (1, gin_o)):
            @pl.when(is_mid)
            def _():
                cm(a, p).wait_send()
                co(a, p, ref).wait_send()
                cl(a, p, ref).wait()

            @pl.when(is_end)
            def _():
                ce(a, p).wait_send()
                co(a, p, ref).wait_recv()

        return keep

    lax.fori_loop(0, n_piece, finish_line, 0)


def comm_call(hidden, cot, tokens, ctx, gj, gain, bias_sum, qkv_w, out_w, gate_w, up_w, down_w):
    rows, width = hidden.shape
    hd = ctx.shape[1]
    ff = gate_w.shape[1]
    full, tail = ff // W, ff % W
    n_out, n_qkv = hd // W, qkv_w.shape[1] // W
    n_batch = n_out + full + 1 + n_qkv + 2 * full + 1
    n_z = 2 * (rows // PR)
    dims = (rows, width, full, tail, n_out, n_qkv, n_batch)
    piece = (W // 2, W)
    vm, dma = pltpu.VMEM, pltpu.SemaphoreType.DMA
    any_spec = pl.BlockSpec(memory_space=pl.ANY)
    vm_spec = pl.BlockSpec(memory_space=pltpu.VMEM)
    return pl.pallas_call(
        functools.partial(comm_kernel, dims),
        out_shape=(
            jax.ShapeDtypeStruct((rows, width), BF),
            jax.ShapeDtypeStruct((rows, width), BF),
            jax.ShapeDtypeStruct((8, width), F32),
            jax.ShapeDtypeStruct((n_batch, 2) + piece, F32),
        ),
        in_specs=[any_spec] * 5 + [vm_spec] * 2 + [any_spec] * 5,
        out_specs=(any_spec, any_spec, vm_spec, any_spec),
        scratch_shapes=[
            vm((4, 2, W, rows), BF),
            vm((rows, width), BF),
            vm((2, rows, width // 2), BF),
            vm((rows, width), BF),
            vm((rows, hd), BF),
            vm((2 * n_qkv, rows, W // 2), BF),
            vm((width, W), BF),
            vm((width, W), BF),
            vm((W, width), BF),
            vm((rows, width), F32),
            vm((full + 1, 2, rows, W), BF),
            vm((4, 2, 2, 2) + piece, BF),
            vm((4, 2, 2, 2) + piece, BF),
            vm((n_batch, 2, 2, 2) + piece, BF),
            vm((n_batch, 2, 2) + piece, BF),
            vm((n_batch, 2) + piece, BF),
            vm((2, rows, width), BF),
            vm((2, rows, width), BF),
            vm((2, rows, width), BF),
            vm((2, 2) + piece, F32),
            vm((5, 8, width), F32),
            vm((4, 8, width), F32),
            vm((2, 2, 8, width), F32),
            dma((13,)),
            dma((3,)),
            dma((4,)),
            dma((n_batch,)),
            dma((n_batch, 2)),
            dma((n_batch, 2)),
            dma((n_batch, 2)),
            dma((n_batch, 2)),
            dma((n_z,)),
            dma((n_z,)),
            dma((n_z,)),
            dma((n_z,)),
            dma((n_z,)),
            dma((n_z,)),
            dma((n_z,)),
            dma((2,)),
            dma((7,)),
            dma((7,)),
        ],
        compiler_params=pltpu.CompilerParams(
            collective_id=0, has_side_effects=True, vmem_limit_bytes=67043328
        ),
        name="ffn_and_sums",
    )(hidden, cot, tokens, ctx, gj, gain[None, :], bias_sum, qkv_w, out_w, gate_w, up_w, down_w)


QB = 128


def attn_kernel(
    heads_scale, tok, seg_ref, gain_ref, shift_ref, freq_ref, w_ref, b_ref, ow_ref, cot,
    hid, ctx_o, gj_o, bias_o,
    bias_m, tab,
):
    rows = tok.shape[0]
    nq = rows // QB
    half = ROT // 2

    @pl.when(pl.program_id(0) == 0)
    def _():
        def norm_step(n, keep):
            r = pl.ds(pl.multiple_of(n * 64, 64), 64)
            v = tok[r, :].astype(F32)
            v = v - jnp.mean(v, -1, keepdims=True)
            v = v * lax.rsqrt(jnp.mean(v * v, -1, keepdims=True) + EPSILON)
            hid[r, :] = (v * gain_ref[...].astype(F32) + shift_ref[...].astype(F32)).astype(BF)
            return keep

        lax.fori_loop(0, rows // 64, norm_step, 0)
        seg = seg_ref[...].astype(F32)
        seg_t = jnp.broadcast_to(seg, (8, rows)).T
        lane = lax.broadcasted_iota(jnp.int32, (QB, QB), 1)
        head_lane = lane % DH
        for i in range(nq):
            lo = max(0, i - 2) * QB
            n = (i + 1) * QB - lo
            q_at = lax.broadcasted_iota(jnp.int32, (QB, n), 0) + i * QB
            k_at = lax.broadcasted_iota(jnp.int32, (QB, n), 1) + lo
            same = seg_t[i * QB : (i + 1) * QB, 0:1] == seg[:, lo : lo + n]
            allowed = same & (q_at >= k_at)
            bias_m[i, :, 0:n] = jnp.where(allowed, 0.0, NEGATIVE)
            place = jnp.sum(jnp.where(allowed, 1.0, 0.0), -1, keepdims=True) - 1.0
            angle = place * freq_ref[...]
            cosine, sine = jnp.cos(angle), jnp.sin(angle)
            for blk in range(3):
                live = head_lane < ROT
                if blk == 1:
                    live = live & (lane >= DH)
                if blk == 2:
                    live = live & (lane < DH)
                scale = jnp.ones((QB, QB), F32)
                if blk == 0:
                    scale = jnp.where(lane < DH, heads_scale, 1.0)
                if blk == 1:
                    scale = jnp.where(lane >= DH, heads_scale, 1.0)
                r = slice(i * QB, (i + 1) * QB)
                tab[blk, 0, r] = jnp.where(live, cosine, 1.0) * scale
                tab[blk, 1, r] = jnp.where(live & (head_lane < half), -sine, 0.0) * scale
                tab[blk, 2, r] = jnp.where(live & (head_lane >= half), sine, 0.0) * scale

    def dot_t(a, b):
        return lax.dot_general(a, b, (((1,), (1,)), ((), ())), preferred_element_type=F32)

    def dot(a, b):
        return jnp.dot(a, b, preferred_element_type=F32)

    joined = dot(hid[...], w_ref[...]) + b_ref[...].astype(F32)
    turned = []
    for blk in range(3):
        v = joined[:, blk * QB : (blk + 1) * QB]
        v = v * tab[blk, 0] + pltpu.roll(v, QB - half, 1) * tab[blk, 1] + pltpu.roll(v, half, 1) * tab[blk, 2]
        turned.append(v.astype(BF))
    gctx = dot_t(cot[...], ow_ref[...]).astype(BF)
    lo_h, hi_h = slice(0, DH), slice(DH, 2 * DH)
    heads = (
        (turned[0][:, lo_h], turned[0][:, hi_h], turned[1][:, lo_h], gctx[:, lo_h]),
        (turned[1][:, hi_h], turned[2][:, lo_h], turned[2][:, hi_h], gctx[:, hi_h]),
    )
    grads, contexts = [], []
    for q, k, v, gc in heads:
        probs, grad_s, out, grad_q = [], [], [], []
        for i in range(nq):
            lo = max(0, i - 2) * QB
            hi = (i + 1) * QB
            s = dot_t(q[i * QB : hi], k[lo:hi]) + bias_m[i, :, 0 : hi - lo]
            e = jnp.exp(s - jnp.max(s, -1, keepdims=True))
            p = e * (1.0 / jnp.sum(e, -1, keepdims=True))
            pb = p.astype(BF)
            out.append(dot(pb, v[lo:hi]))
            gp = dot_t(gc[i * QB : hi], v[lo:hi])
            gs = (p * (gp - jnp.sum(p * gp, -1, keepdims=True))).astype(BF)
            grad_q.append(dot(gs, k[lo:hi]))
            probs.append(pb)
            grad_s.append(gs)
        grad_k, grad_v = [], []
        for j in range(nq):
            top = min(j + 3, nq)

            def stack(parts):
                cut = []
                for i in range(j, top):
                    at = (j - max(0, i - 2)) * QB
                    cut.append(parts[i][:, at : at + QB].T)
                return jnp.concatenate(cut, 1)

            grad_k.append(dot(stack(grad_s), q[j * QB : top * QB]))
            grad_v.append(dot(stack(probs), gc[j * QB : top * QB]))
        contexts.append(jnp.concatenate(out, 0))
        grads.append([jnp.concatenate(part, 0) for part in (grad_q, grad_k, grad_v)])
    ctx_o[...] = jnp.concatenate(contexts, 1).astype(BF)
    (q0, k0, v0), (q1, k1, v1) = grads
    for blk, pair in enumerate(((q0, k0), (v0, q1), (k1, v1))):
        g = jnp.concatenate(pair, 1)
        g = g * tab[blk, 0] - pltpu.roll(g, QB - half, 1) * tab[blk, 1] - pltpu.roll(g, half, 1) * tab[blk, 2]
        g = g.astype(BF)
        gj_o[blk] = g
        bias_o[:, blk * QB : (blk + 1) * QB] = jnp.sum(g.astype(F32), 0, keepdims=True)


def attn_call(tokens, segment_ids, gain, shift, qkv_w, qkv_b, out_w, cot):
    rows, width = tokens.shape
    hd = out_w.shape[0]
    steps = hd // (2 * DH)
    three = 3 * QB
    lane = jnp.arange(QB) % DH % (ROT // 2)
    freq = jnp.power(10000.0, -2.0 * lane.astype(F32) / ROT)[None, :]
    whole = lambda shape: pl.BlockSpec(shape, lambda i: (0,) * len(shape))
    once = lambda shape: pl.BlockSpec(shape, lambda i: (0,) * len(shape), pipeline_mode=pl.Buffered(1))
    return pl.pallas_call(
        functools.partial(attn_kernel, DH ** (-0.5)),
        grid=(steps,),
        out_shape=(
            jax.ShapeDtypeStruct((rows, width), BF),
            jax.ShapeDtypeStruct((rows, hd), BF),
            jax.ShapeDtypeStruct((3 * steps, rows, QB), BF),
            jax.ShapeDtypeStruct((1, 3 * hd), F32),
        ),
        in_specs=[
            once((rows, width)),
            whole((1, rows)),
            whole((1, width)),
            whole((1, width)),
            whole((1, QB)),
            pl.BlockSpec((width, three), lambda i: (0, i)),
            pl.BlockSpec((1, three), lambda i: (0, i)),
            pl.BlockSpec((QB, width), lambda i: (i, 0)),
            once((rows, width)),
        ],
        out_specs=(
            whole((rows, width)),
            pl.BlockSpec((rows, QB), lambda i: (0, i)),
            pl.BlockSpec((3, rows, QB), lambda i: (i, 0, 0)),
            pl.BlockSpec((1, three), lambda i: (0, i)),
        ),
        scratch_shapes=[pltpu.VMEM((rows // QB, QB, three), F32), pltpu.VMEM((3, 3, rows, QB), F32)],
        compiler_params=pltpu.CompilerParams(vmem_limit_bytes=60 << 20),
        name="attention",
    )(tokens, segment_ids, gain[None, :], shift[None, :], freq, qkv_w, qkv_b[None, :], out_w, cot)


def fast(
    n_dp,
    n_tensor,
    tokens,
    segment_ids,
    norm_gain,
    norm_bias,
    qkv_weight,
    qkv_bias,
    out_weight,
    gate_weight,
    up_weight,
    down_weight,
    cotangent,
):
    args = (tokens, segment_ids, norm_gain, norm_bias, qkv_weight, qkv_bias, out_weight, gate_weight, up_weight, down_weight, cotangent)
    row_count, width = tokens.shape
    ff = gate_weight.shape[1]
    fits = (
        (n_dp, n_tensor) == (8, 4)
        and segment_ids.shape == (1, row_count)
        and (row_count, width) == (512, 8 * W)
        and ff % W == W // 2
        and qkv_weight.shape[1] % W == 0
        and out_weight.shape[0] % W == 0
        and qkv_weight.shape[1] == 3 * out_weight.shape[0]
        and 2 * DH == QB
    )
    if not fits:
        return local(*args)
    hidden_in, context, grad_joined, bias_local = attn_call(
        tokens, segment_ids, norm_gain, norm_bias, qkv_weight, qkv_bias, out_weight, cotangent
    )
    output, grad_input, small, sums = comm_call(
        hidden_in, cotangent, tokens, context, grad_joined, norm_gain, bias_local,
        qkv_weight, out_weight, gate_weight, up_weight, down_weight,
    )
    full, tail = ff // W, ff % W
    n_out, n_qkv = out_weight.shape[0] // W, qkv_weight.shape[1] // W
    n_batch = sums.shape[0]
    b0 = n_out + full
    b1 = b0 + 1 + n_qkv
    flat = sums.reshape(n_batch, W, W)

    def side(first, count, step):
        return [flat[first + step * i] for i in range(count)]

    last = flat[n_batch - 1]
    tail_down = sums[b0, :, : tail // 2, :].reshape(tail, W)
    return (
        output,
        grad_input,
        small[0],
        small[1],
        jnp.concatenate(side(b0 + 1, n_qkv, 1), 1),
        small[2, : n_qkv * W],
        jnp.concatenate(side(0, n_out, 1), 0),
        jnp.concatenate(side(b1, full, 2) + [last[:, :tail]], 1),
        jnp.concatenate(side(b1 + 1, full, 2) + [last[:, tail:]], 1),
        jnp.concatenate(side(n_out, full, 1) + [tail_down], 0),
    )


def solution(mesh):
    body = functools.partial(fast, mesh.shape["dp"], mesh.shape["tensor"])
    return jax.shard_map(
        body,
        mesh=mesh,
        in_specs=(
            P("dp", None),
            P("dp", None),
            P(),
            P(),
            P(None, "tensor"),
            P("tensor"),
            P("tensor", None),
            P(None, "tensor"),
            P(None, "tensor"),
            P("tensor", None),
            P("dp", None),
        ),
        out_specs=(
            P("dp", None),
            P("dp", None),
            P(),
            P(),
            P("dp", "tensor"),
            P("tensor"),
            P("tensor", "dp"),
            P("dp", "tensor"),
            P("dp", "tensor"),
            P("tensor", "dp"),
        ),
        check_vma=False,
    )
```

profile of v0, /device:TPU:0, one launch (start us, length us, event | category | flops | bytes accessed | tf_op | source)
XLA Modules:
  0.0 213.1 jit_solution(4149527469723827403)
XLA Ops:
  0.6 0.5 fusion.2.freq_ref
  1.2 1.3 broadcast_in_dim.13.b_ref
  2.5 1.3 broadcast_in_dim.11.gain_ref
  3.7 1.3 broadcast_in_dim.12.shift_ref
  5.0 38.9 %attention.1 = (bf16[512,2048]{1,0:T(8,128)(2,1)}, bf16[512,512]{1,0:T(8,128)(2,1)}, bf16[12,512,128]{2,1,0:T(8,128)(2,1)}, f32[1,1536]{1,0:T(1,128)}) custom-call(bf16[512,2048]{1,0:T(8,128)(2,1)} %tok_h.1, s32[1,512]{1,0:T(1,128)} %seg_ref.1, bf16[1,2048]{1,0:T(2,128)(2,1)} %broadcast_in_dim.11.gain_ref, bf16[1,2048]{1,0:T(2,128)(2,1)} %broadcast_in_dim.12.shift_ref, ...), custom_call_target="tpu_custom_call" | custom-call | tf_op jit(solution)/shard_map/attention/pallas_call | solution.py:1023
  43.9 152.1 %ffn_and_sums.1 = (bf16[512,2048]{1,0:T(8,128)(2,1)}, bf16[512,2048]{1,0:T(8,128)(2,1)}, f32[8,2048]{1,0:T(8,128)}, f32[25,2,128,256]{3,2,1,0:T(8,128)}) custom-call(bf16[512,2048]{1,0:T(8,128)(2,1)} %get-tuple-element.18.hid_h, bf16[512,2048]{1,0:T(8,128)(2,1)} %cot_h.1, bf16[512,2048]{1,0:T(8,128)(2,1)} %tok_h.1, ...), custom_call_target="tpu_custom_call" | custom-call | tf_op jit(solution)/shard_map/ffn_and_sums/pallas_call | solution.py:841
  196.1 1.4 slice_reduce_fusion
  197.5 1.5 fusion.6
  199.0 0.9 slice.143
  199.9 1.4 fusion.5
  201.3 2.7 %fusion.4 = (f32[1,2,128,256]{3,2,1,0:T(8,128)S(1)}, f32[1,2,128,256]{3,2,1,0:T(8,128)S(1)}, f32[1,2,128,256]{3,2,1,0:T(8,128)S(1)}, f32[1,2,128,256]{3,2,1,0:T(...) fusion(f32[25,2,128,256]{3,2,1,0:T(8,128)} %get-tuple-element.25), kind=kLoop, calls=%fused_computation.34 | loop fusion | bytes 9961472 | tf_op jit(solution)/shard_map/slice | solution.py:1100
  204.0 0.8 pad_maximum_fusion
  205.0 0.0 copy-start.2
  205.2 0.9 copy-done.2
  206.2 0.0 copy-start.3
  206.2 0.0 copy-start.4
  206.3 0.0 copy-start.1
  206.5 0.9 copy-done.3
  207.3 0.5 copy-done.4
  207.8 1.1 copy-done.1
  208.9 0.0 copy-start.5
  208.9 0.0 copy-start
  208.9 1.3 copy.43
  210.2 0.5 copy-done.5
  210.7 1.0 copy-done
  211.8 1.3 copy.44
  (22 shorter events, 0.5 us)
Async XLA Ops:
  205.0 1.1 copy-start.2
  206.2 1.1 copy-start.3
  206.2 1.6 copy-start.4
  206.3 2.6 %copy-start.1 = (bf16[512,2048]{1,0:T(8,128)(2,1)S(1)}, bf16[512,2048]{1,0:T(8,128)(2,1)}, u32[]{:S(2)}) copy-start(bf16[512,2048]{1,0:T(8,128)(2,1)} %get-tuple-element.66) | copy-start | bytes 6291460
  208.9 1.9 copy-start.5
  208.9 2.9 %copy-start = (bf16[512,2048]{1,0:T(8,128)(2,1)S(1)}, bf16[512,2048]{1,0:T(8,128)(2,1)}, u32[]{:S(2)}) copy-start(bf16[512,2048]{1,0:T(8,128)(2,1)} %get-tuple-element.67) | copy-start | bytes 6291460
where the time goes:
time: 214 us; the launch traced here: 213 us
  Pallas kernels  191 us (89%)
  local copies, waits for them, and re-layouts  19.8 us (9%)
    pallas_call x1, Pallas kernels, comm_call(): pl.pallas_call(functools.partial(comm_kernel, dims), out_shape=(jax.Shape...  152 us
    pallas_call x1, Pallas kernels, attn_call(): pl.pallas_call(functools.partial(attn_kernel, DH ** (-0.5)), grid=(steps,...  38.9 us
    unnamed x33, local copies, waits for them, and re-layouts  8.01 us

commit v1 on v0

--- a/solution.py
+++ b/solution.py
@@ -251,20 +251,26 @@
 W = 256
 PR = 32
 SMALL_AT = 2
+LATE = 4
 
 
 def comm_kernel(
     dims,
     hid_h, cot_h, tok_h, ctx_h, gj_h, gain_ref, bias_ref, qkv_h, out_h, gate_h, up_h, down_h,
-    out_o, gin_o, sv_o, sums_o,
+    out_o, gin_o, sv_o, gq_o, go_o, gg_o, gu_o, gd_o,
     hid_t, cot, cot_s, tok, ctx, gj, w_a, w_b, w_d, acc, gu, s1, own, recv1, recv2, recv3,
-    zs, ze, zm, stage, svb, svr, svq,
+    zs, ze, zm, svb, svr, svq,
     ld_sem, w_sem, s1_send, s1_recv, s2_send, s2_recv, s3_send, s3_recv,
-    e_send, e_recv, m_send, m_recv, o_send, o_recv, o_loc, st_sem, v_send, v_recv,
+    e_send, e_recv, m_send, m_recv, o_send, o_recv, o_loc, g_sem, v_send, v_recv,
 ):
     rows, width, full, tail, n_out, n_qkv, n_batch = dims
     n_piece = rows // PR
     hid = zs.at[1]
+    early = full // 2
+    t0 = full * W
+    b_tail_down = n_out + early
+    b_pairs = n_out + n_qkv + 1
+    b_up = b_pairs + 2 * full
     dp = lax.axis_index("dp")
     zi = lax.axis_index("tensor")
     c = lax.rem(dp, 2)
@@ -296,10 +302,9 @@
     def w_up(i):
         return pltpu.make_async_copy(up_h.at[:, pl.ds(i * W, W)], w_b, w_sem.at[1])
 
-    def w_qkv(j):
-        return pltpu.make_async_copy(qkv_h.at[:, pl.ds(j * W, W)], w_a, w_sem.at[0])
-
-    t0 = full * W
+    def w_qkv(j, side):
+        return pltpu.make_async_copy(qkv_h.at[:, pl.ds(j * W, W)], (w_a, w_b)[side], w_sem.at[side])
+
     w_gate_t = pltpu.make_async_copy(gate_h.at[:, pl.ds(t0, tail)], w_a.at[:, 0:tail], w_sem.at[0])
     w_up_t = pltpu.make_async_copy(up_h.at[:, pl.ds(t0, tail)], w_a.at[:, tail : 2 * tail], w_sem.at[1])
     w_down_t = pltpu.make_async_copy(down_h.at[pl.ds(t0, tail), :], w_d.at[0:tail, :], w_sem.at[2])
@@ -381,22 +386,46 @@
         c3(b, 0).start()
         c3(b, 1).start()
 
-    def st_copy(b):
-        slot = lax.rem(b, 2)
-        return pltpu.make_async_copy(stage.at[slot], sums_o.at[b], st_sem.at[slot])
+    def cut(b, h, ref, row, col, n=W // 2, lo=0, wide=W):
+        if not isinstance(row, int):
+            row = pl.multiple_of(row, 64)
+        if not isinstance(col, int):
+            col = pl.multiple_of(col, W // 2)
+        return pltpu.make_async_copy(
+            recv3.at[b, h, 0:n, lo : lo + wide], ref.at[pl.ds(row + h * n, n), pl.ds(col, wide)], g_sem.at[b, h]
+        )
+
+    groups = (
+        (0, n_out, 1, lambda b, h, i: (cut(b, h, go_o, i * W, 0),)),
+        (n_out, early, 1, lambda b, h, i: (cut(b, h, gq_o, 0, i * W),)),
+        (b_tail_down, 1, 1, lambda b, h, i: (cut(b, h, gd_o, t0, 0, tail // 2),)),
+        (b_tail_down + 1, n_qkv - early, 1, lambda b, h, i: (cut(b, h, gq_o, 0, (i + early) * W),)),
+        (b_pairs, full, 2, lambda b, h, i: (cut(b, h, gd_o, i * W, 0),)),
+        (b_pairs + 1, full, 2, lambda b, h, i: (cut(b, h, gg_o, 0, i * W),)),
+        (b_up, full, 1, lambda b, h, i: (cut(b, h, gu_o, 0, i * W),)),
+        (
+            b_up + full, 1, 1,
+            lambda b, h, i: (
+                cut(b, h, gg_o, 0, t0, wide=tail), cut(b, h, gu_o, 0, t0, lo=tail, wide=tail)
+            ),
+        ),
+    )
 
     def ev3(b):
-        slot = lax.rem(b, 2)
         c3(b, 0).wait_recv()
         c3(b, 1).wait_recv()
-
-        @pl.when(b >= 2)
-        def _():
-            st_copy(b - 2).wait()
-
-        stage[slot, 0] = up32(recv2[b, 0, y]) + up32(recv3[b, 0])
-        stage[slot, 1] = up32(recv2[b, 1, x]) + up32(recv3[b, 1])
-        st_copy(b).start()
+        recv3[b, 0] += recv2[b, 0, y]
+        recv3[b, 1] += recv2[b, 1, x]
+        for first, count, step, make in groups:
+            here = (b >= first) & (b < first + count * step)
+            if step > 1:
+                here = here & (lax.rem(b - first, step) == 0)
+
+            @pl.when(here)
+            def _(first=first, step=step, make=make):
+                for h in range(2):
+                    for cp in make(b, h, (b - first) // step):
+                        cp.start()
 
     def before_put(b):
         @pl.when(b >= 4)
@@ -405,10 +434,6 @@
 
     def after_put(b):
         c1(b).start()
-
-        @pl.when(b >= 2)
-        def _():
-            ev1(b - 2)
 
     def put_rows(b, grad):
         slot = lax.rem(b, 4)
@@ -531,6 +556,11 @@
     def act_of(g, u):
         return (g * jax.nn.sigmoid(g) * u).astype(BF)
 
+    def joined_grad(j):
+        return jnp.concatenate([gj[2 * j], gj[2 * j + 1]], axis=1)
+
+    gj_ld.wait()
+
     def fwd(i, keep):
         w_gate(i).wait()
         g = jnp.dot(hid[...], w_a[...], preferred_element_type=F32)
@@ -550,6 +580,17 @@
         gu[i, 0] = g.astype(BF)
         gu[i, 1] = u.astype(BF)
         mixed = act_of(g, u)
+
+        @pl.when(i == 0)
+        def _():
+            for b in range(n_out):
+                ev1(jnp.int32(b))
+
+        @pl.when((i >= 2) & (lax.rem(i, 2) == 0))
+        def _():
+            ev1(n_out + i // 2 - 1)
+            ev2(i // 2 - 1)
+
         w_down(i).wait()
         acc_cols(mixed, w_d, W, False)
 
@@ -561,21 +602,23 @@
         def _():
             w_down_t.start()
 
-        put_cols(n_out + i, mixed.T)
+        @pl.when(lax.rem(i, 2) == 1)
+        def _():
+            put_rows(n_out + i // 2, joined_grad(i // 2))
+
         return keep
 
     lax.fori_loop(0, full, fwd, 0)
     w_gate_t.wait()
     w_up_t.wait()
+    w_qkv(1, 1).start()
     both = jnp.dot(hid[...], w_a[...], preferred_element_type=F32)
-    gj_ld.wait()
-    w_qkv(0).start()
+    w_qkv(0, 0).start()
     gu[full, 0] = both.astype(BF)
     mixed = act_of(both[:, 0:tail], both[:, tail:])
     w_down_t.wait()
     acc_cols(mixed, w_d, tail, False)
     w_down(0).start()
-    b0 = n_out + full
 
     tok_ld.wait()
     cot_ld.wait()
@@ -665,33 +708,41 @@
             lax.fori_loop(0, n_piece, send, 0)
 
     to_line(0)
-    put_cols(jnp.int32(b0), mixed.T)
-    b0 = b0 + 1
-
-    def joined(j, keep):
-        grad = jnp.concatenate([gj[2 * j], gj[2 * j + 1]], axis=1)
-        w_qkv(j).wait()
-        acc_rows(grad, w_a)
-
-        @pl.when(j + 1 < n_qkv)
-        def _():
-            w_qkv(j + 1).start()
-
-        @pl.when(j + 1 == n_qkv)
-        def _():
-            w_gate(0).start()
-            w_up(0).start()
-
-        put_rows(b0 + j, grad)
-
-        @pl.when((j >= 3) & (lax.rem(j, 2) == 1))
-        def _():
-            ev_e((j - 3) // 2)
+    put_cols(jnp.int32(b_tail_down), mixed.T)
+
+    def joined(n, keep):
+        for side in range(2):
+            j = 2 * n + side
+            w_qkv(j, side).wait()
+            acc_rows(joined_grad(j), (w_a, w_b)[side])
+
+            @pl.when(j + 2 < n_qkv)
+            def _(j=j, side=side):
+                w_qkv(j + 2, side).start()
+
+            @pl.when(j + 2 >= n_qkv)
+            def _(side=side):
+                (w_gate, w_up)[side](0).start()
+
+            @pl.when(j + early < n_qkv)
+            def _(j=j):
+                b = b_tail_down + 1 + j
+                put_rows(b, joined_grad(j + early))
+                ev1(b - 1)
+
+        ev_e(n)
+
+        @pl.when(n == 1)
+        def _():
+            ev2(jnp.int32(early))
+
+        @pl.when(n >= 2)
+        def _():
+            ev_m(n - 2)
 
         return keep
 
-    lax.fori_loop(0, n_qkv, joined, 0)
-    b1 = b0 + n_qkv
+    lax.fori_loop(0, n_qkv // 2, joined, 0)
 
     def gate_grads(gm, g, u):
         sg = jax.nn.sigmoid(g)
@@ -702,7 +753,7 @@
     def cols_t(left, w_ref, k):
         return lax.dot_general(left, w_ref[0:k, :], (((1,), (1,)), ((), ())), preferred_element_type=F32)
 
-    e0 = (n_qkv - 2) // 2
+    e0 = n_qkv // 2
 
     def bwd(i, keep):
         w_down(i).wait()
@@ -716,7 +767,11 @@
         def _():
             w_down_t.start()
 
-        g_gate, g_up = gate_grads(gm, up32(gu[i, 0]), up32(gu[i, 1]))
+        g, u = up32(gu[i, 0]), up32(gu[i, 1])
+        mixed = act_of(g, u)
+        g_gate, g_up = gate_grads(gm, g, u)
+        gu[i, 0] = g_gate
+        gu[i, 1] = g_up
         w_gate(i).wait()
         acc_rows(g_gate, w_a)
         w_up(i).wait()
@@ -732,11 +787,18 @@
             w_gate_t.start()
             w_up_t.start()
 
-        for half, grad in enumerate((g_gate, g_up)):
-            put_rows(b1 + 2 * i + half, grad)
-            ev_e(e0 + 2 * i + half)
-            ev2(2 * i + half)
-            ev_m(e0 - 2 + 2 * i + half)
+        b = b_pairs + 2 * i
+        e = e0 + 2 * i
+        put_cols(b, mixed.T)
+        ev1(b - 1)
+        ev2(early + 1 + 2 * i)
+        ev_e(e)
+        ev_m(e - 2)
+        put_rows(b + 1, gu[i, 0])
+        ev1(b)
+        ev2(early + 2 + 2 * i)
+        ev_e(e + 1)
+        ev_m(e - 1)
         return keep
 
     lax.fori_loop(0, full, bwd, 0)
@@ -745,24 +807,36 @@
     both = up32(gu[full, 0])
     g_gate, g_up = gate_grads(gm, both[:, 0:tail], both[:, tail:])
     both = jnp.concatenate([g_gate, g_up], axis=1)
+    gu[full, 0] = both
     w_gate_t.wait()
     w_up_t.wait()
     acc_rows(both, w_a)
     svb[0] = jnp.zeros_like(svb[0])
     svb[0, 2:3, 0 : n_qkv * W] = bias_ref[...]
     to_line(1)
-    b2 = b1 + 2 * full
+
     e0 = e0 + 2 * full
-    put_rows(jnp.int32(b2), both)
-    ev_e(jnp.int32(e0))
-    ev_m(jnp.int32(e0 - 2))
-    ev1(jnp.int32(b2 - 1))
-    ev1(jnp.int32(b2))
+
+    def left_over(i, keep):
+        b = b_up + i
+        at = jnp.where(i == full, 0, 1)
+        put_rows(b, gu[i, at])
+        ev1(b - 1)
+
+        @pl.when(lax.rem(i, 2) == 0)
+        def _():
+            ev2(early + 1 + 2 * full + i // 2)
+            ev_e(e0 + i // 2)
+            ev_m(e0 + i // 2 - 2)
+
+        return keep
+
+    lax.fori_loop(0, full + 1, left_over, 0)
+    ev1(jnp.int32(n_batch - 1))
+    e0 = e0 + (full + 2) // 2
 
     n_e = 2 * n_piece
-    e0 = e0 + 1
-    two = 2 * full
-    late = 7
+    two = early + 1 + 2 * full + (full + 2) // 2
     smalls = (small_1, small_2, small_3, small_4)
 
     def drain(k, keep):
@@ -782,7 +856,7 @@
             pl.when(k == SMALL_AT + i)(small)
 
         for h in range(2):
-            b = 2 * (k - late) + h
+            b = 2 * (k - LATE) + h
 
             @pl.when((b >= 0) & (b < n_batch))
             def _():
@@ -790,7 +864,7 @@
 
         return keep
 
-    lax.fori_loop(0, max(late + (n_batch + 1) // 2, n_e - e0 + 2), drain, 0)
+    lax.fori_loop(0, max(LATE + (n_batch + 1) // 2, n_e - e0 + 2), drain, 0)
     small_5()
 
     small_sent()
@@ -804,8 +878,11 @@
     lax.fori_loop(0, n_batch, finish, 0)
     for k in range(4):
         c1(jnp.int32(n_batch - 4 + k)).wait_send()
-    for k in range(2):
-        st_copy(jnp.int32(n_batch - 2 + k)).wait()
+    for first, count, step, make in groups:
+        for i in range(count):
+            for h in range(2):
+                for cp in make(first + i * step, h, i):
+                    cp.wait()
 
     def finish_line(p, keep):
         for a, ref in ((0, out_o), (1, gin_o)):
@@ -844,10 +921,14 @@
             jax.ShapeDtypeStruct((rows, width), BF),
             jax.ShapeDtypeStruct((rows, width), BF),
             jax.ShapeDtypeStruct((8, width), F32),
-            jax.ShapeDtypeStruct((n_batch, 2) + piece, F32),
+            jax.ShapeDtypeStruct((W, n_qkv * W), BF),
+            jax.ShapeDtypeStruct((hd, W), BF),
+            jax.ShapeDtypeStruct((W, ff), BF),
+            jax.ShapeDtypeStruct((W, ff), BF),
+            jax.ShapeDtypeStruct((ff, W), BF),
         ),
         in_specs=[any_spec] * 5 + [vm_spec] * 2 + [any_spec] * 5,
-        out_specs=(any_spec, any_spec, vm_spec, any_spec),
+        out_specs=(any_spec, any_spec, vm_spec) + (any_spec,) * 5,
         scratch_shapes=[
             vm((4, 2, W, rows), BF),
             vm((rows, width), BF),
@@ -868,7 +949,6 @@
             vm((2, rows, width), BF),
             vm((2, rows, width), BF),
             vm((2, rows, width), BF),
-            vm((2, 2) + piece, F32),
             vm((5, 8, width), F32),
             vm((4, 8, width), F32),
             vm((2, 2, 8, width), F32),
@@ -887,7 +967,7 @@
             dma((n_z,)),
             dma((n_z,)),
             dma((n_z,)),
-            dma((2,)),
+            dma((n_batch, 2)),
             dma((7,)),
             dma((7,)),
         ],
@@ -899,12 +979,13 @@
 
 
 QB = 128
+ROWS = 32
 
 
 def attn_kernel(
     heads_scale, tok, seg_ref, gain_ref, shift_ref, freq_ref, w_ref, b_ref, ow_ref, cot,
     hid, ctx_o, gj_o, bias_o,
-    bias_m, tab,
+    bias_m, tab, s_m, g_m, p_m, gs_m,
 ):
     rows = tok.shape[0]
     nq = rows // QB
@@ -970,35 +1051,41 @@
         (turned[0][:, lo_h], turned[0][:, hi_h], turned[1][:, lo_h], gctx[:, lo_h]),
         (turned[1][:, hi_h], turned[2][:, lo_h], turned[2][:, hi_h], gctx[:, hi_h]),
     )
-    grads, contexts = [], []
-    for q, k, v, gc in heads:
-        probs, grad_s, out, grad_q = [], [], [], []
-        for i in range(nq):
-            lo = max(0, i - 2) * QB
-            hi = (i + 1) * QB
-            s = dot_t(q[i * QB : hi], k[lo:hi]) + bias_m[i, :, 0 : hi - lo]
+    spans = [(max(0, i - 2) * QB, (i + 1) * QB) for i in range(nq)]
+    blocks = [(n, i) for i in range(nq) for n in range(2)]
+    for n, i in blocks:
+        q, k, v, gc = heads[n]
+        lo, hi = spans[i]
+        s_m[n, i, :, 0 : hi - lo] = dot_t(q[i * QB : hi], k[lo:hi])
+        g_m[n, i, :, 0 : hi - lo] = dot_t(gc[i * QB : hi], v[lo:hi])
+    for n, i in blocks:
+        lo, hi = spans[i]
+        for r in range(0, QB, ROWS):
+            rr = slice(r, r + ROWS)
+            s = s_m[n, i, rr, 0 : hi - lo] + bias_m[i, rr, 0 : hi - lo]
             e = jnp.exp(s - jnp.max(s, -1, keepdims=True))
             p = e * (1.0 / jnp.sum(e, -1, keepdims=True))
-            pb = p.astype(BF)
-            out.append(dot(pb, v[lo:hi]))
-            gp = dot_t(gc[i * QB : hi], v[lo:hi])
-            gs = (p * (gp - jnp.sum(p * gp, -1, keepdims=True))).astype(BF)
-            grad_q.append(dot(gs, k[lo:hi]))
-            probs.append(pb)
-            grad_s.append(gs)
-        grad_k, grad_v = [], []
+            gp = g_m[n, i, rr, 0 : hi - lo]
+            p_m[n, i, rr, 0 : hi - lo] = p.astype(BF)
+            gs_m[n, i, rr, 0 : hi - lo] = (p * (gp - jnp.sum(p * gp, -1, keepdims=True))).astype(BF)
+    grads, contexts = [], []
+    for n, (q, k, v, gc) in enumerate(heads):
+        out, grad_q, grad_k, grad_v = [], [], [], []
+        for i, (lo, hi) in enumerate(spans):
+            out.append(dot(p_m[n, i, :, 0 : hi - lo], v[lo:hi]))
+            grad_q.append(dot(gs_m[n, i, :, 0 : hi - lo], k[lo:hi]))
         for j in range(nq):
             top = min(j + 3, nq)
 
-            def stack(parts):
+            def stack(part):
                 cut = []
                 for i in range(j, top):
-                    at = (j - max(0, i - 2)) * QB
-                    cut.append(parts[i][:, at : at + QB].T)
+                    at = j * QB - spans[i][0]
+                    cut.append(part[n, i, :, at : at + QB].T)
                 return jnp.concatenate(cut, 1)
 
-            grad_k.append(dot(stack(grad_s), q[j * QB : top * QB]))
-            grad_v.append(dot(stack(probs), gc[j * QB : top * QB]))
+            grad_k.append(dot(stack(gs_m), q[j * QB : top * QB]))
+            grad_v.append(dot(stack(p_m), gc[j * QB : top * QB]))
         contexts.append(jnp.concatenate(out, 0))
         grads.append([jnp.concatenate(part, 0) for part in (grad_q, grad_k, grad_v)])
     ctx_o[...] = jnp.concatenate(contexts, 1).astype(BF)
@@ -1046,7 +1133,14 @@
             pl.BlockSpec((3, rows, QB), lambda i: (i, 0, 0)),
             pl.BlockSpec((1, three), lambda i: (0, i)),
         ),
-        scratch_shapes=[pltpu.VMEM((rows // QB, QB, three), F32), pltpu.VMEM((3, 3, rows, QB), F32)],
+        scratch_shapes=[
+            pltpu.VMEM((rows // QB, QB, three), F32),
+            pltpu.VMEM((3, 3, rows, QB), F32),
+            pltpu.VMEM((2, rows // QB, QB, three), F32),
+            pltpu.VMEM((2, rows // QB, QB, three), F32),
+            pltpu.VMEM((2, rows // QB, QB, three), BF),
+            pltpu.VMEM((2, rows // QB, QB, three), BF),
+        ],
         compiler_params=pltpu.CompilerParams(vmem_limit_bytes=60 << 20),
         name="attention",
     )(tokens, segment_ids, gain[None, :], shift[None, :], freq, qkv_w, qkv_b[None, :], out_w, cot)
@@ -1075,7 +1169,7 @@
         and segment_ids.shape == (1, row_count)
         and (row_count, width) == (512, 8 * W)
         and ff % W == W // 2
-        and qkv_weight.shape[1] % W == 0
+        and qkv_weight.shape[1] % (2 * W) == 0
         and out_weight.shape[0] % W == 0
         and qkv_weight.shape[1] == 3 * out_weight.shape[0]
         and 2 * DH == QB
@@ -1085,33 +1179,22 @@
     hidden_in, context, grad_joined, bias_local = attn_call(
         tokens, segment_ids, norm_gain, norm_bias, qkv_weight, qkv_bias, out_weight, cotangent
     )
-    output, grad_input, small, sums = comm_call(
+    output, grad_input, small, *sums = comm_call(
         hidden_in, cotangent, tokens, context, grad_joined, norm_gain, bias_local,
         qkv_weight, out_weight, gate_weight, up_weight, down_weight,
     )
-    full, tail = ff // W, ff % W
-    n_out, n_qkv = out_weight.shape[0] // W, qkv_weight.shape[1] // W
-    n_batch = sums.shape[0]
-    b0 = n_out + full
-    b1 = b0 + 1 + n_qkv
-    flat = sums.reshape(n_batch, W, W)
-
-    def side(first, count, step):
-        return [flat[first + step * i] for i in range(count)]
-
-    last = flat[n_batch - 1]
-    tail_down = sums[b0, :, : tail // 2, :].reshape(tail, W)
+    joined_w, out_w, gate_w, up_w, down_w = (v.astype(F32) for v in sums)
     return (
         output,
         grad_input,
         small[0],
         small[1],
-        jnp.concatenate(side(b0 + 1, n_qkv, 1), 1),
-        small[2, : n_qkv * W],
-        jnp.concatenate(side(0, n_out, 1), 0),
-        jnp.concatenate(side(b1, full, 2) + [last[:, :tail]], 1),
-        jnp.concatenate(side(b1 + 1, full, 2) + [last[:, tail:]], 1),
-        jnp.concatenate(side(n_out, full, 1) + [tail_down], 0),
+        joined_w,
+        small[2, : qkv_weight.shape[1]],
+        out_w,
+        gate_w,
+        up_w,
+        down_w,
     )
 
 

time: 214 us -> 198 us (0.925)
  Pallas kernels: 191 us -> 179 us
  local copies, waits for them, and re-layouts: 19.8 us -> 10.5 us
  other arithmetic: 1.35 us -> 7.48 us
    pallas_call x1, Pallas kernels: 38.9 us -> 25.8 us  [attn_call(): pl.pallas_call(functools.partial(attn_kernel, DH ** (-0.5)), grid=(steps,...]
    convert_element_type x0 -> x5, other arithmetic: none -> 6.95 us  [fast(): joined_w, out_w, gate_w, up_w, down_w = (v.astype(F32) for v in sums)]
    slice x4 -> x1, local copies, waits for them, and re-layouts: 6.39 us -> 1.42 us  [fast(): small[2, :qkv_weight.shape[1]]]
    unnamed x33 -> x14, local copies, waits for them, and re-layouts: 8.01 us -> 3.68 us
where the time goes in v1:
time: 198 us
  Pallas kernels  179 us (90%)
  local copies, waits for them, and re-layouts  10.5 us (5%)
  other arithmetic  7.48 us (4%)
    pallas_call x1, Pallas kernels, comm_call(): pl.pallas_call(functools.partial(comm_kernel, dims), out_shape=(jax.Shape...  153 us
    pallas_call x1, Pallas kernels, attn_call(): pl.pallas_call(functools.partial(attn_kernel, DH ** (-0.5)), grid=(steps,...  25.8 us
    convert_element_type x5, other arithmetic, fast(): joined_w, out_w, gate_w, up_w, down_w = (v.astype(F32) for v in sums)  6.95 us

profile of v1, /device:TPU:0, one launch (start us, length us, event | category | flops | bytes accessed | tf_op | source)
XLA Modules:
  0.0 197.9 jit_solution(12399828955478758608)
XLA Ops:
  0.6 1.3 broadcast_in_dim.11.gain_ref
  1.9 1.3 broadcast_in_dim.12.shift_ref
  3.2 1.3 broadcast_in_dim.13.b_ref
  4.5 0.5 fusion.2.freq_ref
  5.0 25.8 %attention.1 = (bf16[512,2048]{1,0:T(8,128)(2,1)}, bf16[512,512]{1,0:T(8,128)(2,1)}, bf16[12,512,128]{2,1,0:T(8,128)(2,1)}, f32[1,1536]{1,0:T(1,128)}) custom-call(bf16[512,2048]{1,0:T(8,128)(2,1)} %tok_h.1, s32[1,512]{1,0:T(1,128)} %seg_ref.1, bf16[1,2048]{1,0:T(2,128)(2,1)} %broadcast_in_dim.11.gain_ref, bf16[1,2048]{1,0:T(2,128)(2,1)} %broadcast_in_dim.12.shift_ref, ...), custom_call_target="tpu_custom_call" | custom-call | tf_op jit(solution)/shard_map/attention/pallas_call | solution.py:1110
  30.9 153.4 %ffn_and_sums.1 = (bf16[512,2048]{1,0:T(8,128)(2,1)}, bf16[512,2048]{1,0:T(8,128)(2,1)}, f32[8,2048]{1,0:T(8,128)}, bf16[256,1536]{1,0:T(8,128)(2,1)}, bf16[512,...) custom-call(bf16[512,2048]{1,0:T(8,128)(2,1)} %get-tuple-element.22.hid_h, ...), custom_call_target="tpu_custom_call" | custom-call | tf_op jit(solution)/shard_map/ffn_and_sums/pallas_call | solution.py:918
  184.3 0.0 copy-start.4
  184.3 1.6 fusion.4
  185.9 1.4 slice_reduce_fusion
  187.3 0.0 copy-start.3
  187.3 2.5 %convert_element_type.26 = f32[256,1536]{1,0:T(8,128)} convert(bf16[256,1536]{1,0:T(8,128)(2,1)} %get-tuple-element.29) | non-fusion elementwise | flops 393216 | bytes 2359296 | tf_op jit(solution)/shard_map/convert_element_type | solution.py:1186
  189.8 0.0 copy-done.4
  189.8 0.0 copy-start.2
  189.8 1.2 convert_element_type.28
  191.0 0.0 copy-done.3
  191.0 0.0 copy-start.5
  191.0 0.0 copy-start.1
  191.0 1.2 convert_element_type.29
  192.2 0.0 copy-done.2
  192.2 1.2 convert_element_type.30
  193.4 0.0 copy-done.5
  193.4 0.8 convert_element_type.27
  194.3 0.0 copy-done.1
  194.3 0.0 copy-start
  194.3 1.3 copy.23
  195.6 1.0 copy-done
  196.6 1.3 copy.24
Async XLA Ops:
  184.3 5.5 %copy-start.4 = (bf16[256,1408]{1,0:T(8,128)(2,1)S(1)}, bf16[256,1408]{1,0:T(8,128)(2,1)}, u32[]{:S(2)}) copy-start(bf16[256,1408]{1,0:T(8,128)(2,1)} %get-tuple-element.31) | copy-start | bytes 2162692
  187.3 3.7 %copy-start.3 = (bf16[256,1408]{1,0:T(8,128)(2,1)S(1)}, bf16[256,1408]{1,0:T(8,128)(2,1)}, u32[]{:S(2)}) copy-start(bf16[256,1408]{1,0:T(8,128)(2,1)} %get-tuple-element.32) | copy-start | bytes 2162692
  189.8 2.4 %copy-start.2 = (bf16[1408,256]{1,0:T(8,128)(2,1)S(1)}, bf16[1408,256]{1,0:T(8,128)(2,1)}, u32[]{:S(2)}) copy-start(bf16[1408,256]{1,0:T(8,128)(2,1)} %get-tuple-element.33) | copy-start | bytes 2162692
  191.0 2.4 %copy-start.5 = (bf16[512,256]{1,0:T(8,128)(2,1)S(1)}, bf16[512,256]{1,0:T(8,128)(2,1)}, u32[]{:S(2)}) copy-start(bf16[512,256]{1,0:T(8,128)(2,1)} %get-tuple-element.30) | copy-start | bytes 786436
  191.0 3.2 %copy-start.1 = (bf16[512,2048]{1,0:T(8,128)(2,1)S(1)}, bf16[512,2048]{1,0:T(8,128)(2,1)}, u32[]{:S(2)}) copy-start(bf16[512,2048]{1,0:T(8,128)(2,1)} %get-tuple-element.46) | copy-start | bytes 6291460
  194.3 2.3 %copy-start = (bf16[512,2048]{1,0:T(8,128)(2,1)S(1)}, bf16[512,2048]{1,0:T(8,128)(2,1)}, u32[]{:S(2)}) copy-start(bf16[512,2048]{1,0:T(8,128)(2,1)} %get-tuple-element.47) | copy-start | bytes 6291460

commit v2 on v1

--- a/solution.py
+++ b/solution.py
@@ -251,13 +251,14 @@
 W = 256
 PR = 32
 SMALL_AT = 2
-LATE = 4
+LATE = 8
+WAIT2 = 2
 
 
 def comm_kernel(
     dims,
-    hid_h, cot_h, tok_h, ctx_h, gj_h, gain_ref, bias_ref, qkv_h, out_h, gate_h, up_h, down_h,
-    out_o, gin_o, sv_o, gq_o, go_o, gg_o, gu_o, gd_o,
+    hid_h, cot_h, tok_h, ctx_h, gj_h, z_h, gu_h, gain_ref, bias_ref, qkv_h, gate_h, up_h, down_h,
+    out_o, gin_o, sg_o, ss_o, sb_o, gq_o, go_o, gg_o, gu_o, gd_o,
     hid_t, cot, cot_s, tok, ctx, gj, w_a, w_b, w_d, acc, gu, s1, own, recv1, recv2, recv3,
     zs, ze, zm, svb, svr, svq,
     ld_sem, w_sem, s1_send, s1_recv, s2_send, s2_recv, s3_send, s3_recv,
@@ -266,11 +267,10 @@
     rows, width, full, tail, n_out, n_qkv, n_batch = dims
     n_piece = rows // PR
     hid = zs.at[1]
-    early = full // 2
     t0 = full * W
-    b_tail_down = n_out + early
-    b_pairs = n_out + n_qkv + 1
-    b_up = b_pairs + 2 * full
+    b_pairs = n_out + n_qkv
+    b_left = b_pairs + 2 * full
+    b_up = b_left + 1
     dp = lax.axis_index("dp")
     zi = lax.axis_index("tensor")
     c = lax.rem(dp, 2)
@@ -290,9 +290,6 @@
     def load(src, dst, k):
         return pltpu.make_async_copy(src, dst, ld_sem.at[k])
 
-    def w_out(j):
-        return pltpu.make_async_copy(out_h.at[pl.ds(j * W, W), :], w_d, w_sem.at[2])
-
     def w_down(i):
         return pltpu.make_async_copy(down_h.at[pl.ds(i * W, W), :], w_d, w_sem.at[2])
 
@@ -319,16 +316,21 @@
         for q in range(4)
         for s in range(2)
     ]
+    z_ld = load(z_h, zs.at[0], 13)
+    gu_ld = load(gu_h, gu, 14)
+    z_ld.start()
     ctx_ld.start()
-    w_out(0).start()
     for cp in cs_ld:
         cp.start()
     hid_ld.start()
-    w_gate(0).start()
-    w_up(0).start()
+    w_qkv(0, 0).start()
+    gj_ld.start()
+    w_qkv(1, 1).start()
+    w_down(0).start()
+    tok_ld.start()
     cot_ld.start()
-    gj_ld.start()
-    tok_ld.start()
+    gu_ld.start()
+    acc[...] = jnp.zeros_like(acc)
 
     barrier = pltpu.get_barrier_semaphore()
     for dev in (core_dev, x_dev, y_dev, {"dp": dp + 2 - 4 * x + 4 - 8 * y}):
@@ -397,9 +399,8 @@
 
     groups = (
         (0, n_out, 1, lambda b, h, i: (cut(b, h, go_o, i * W, 0),)),
-        (n_out, early, 1, lambda b, h, i: (cut(b, h, gq_o, 0, i * W),)),
-        (b_tail_down, 1, 1, lambda b, h, i: (cut(b, h, gd_o, t0, 0, tail // 2),)),
-        (b_tail_down + 1, n_qkv - early, 1, lambda b, h, i: (cut(b, h, gq_o, 0, (i + early) * W),)),
+        (n_out, n_qkv, 1, lambda b, h, i: (cut(b, h, gq_o, 0, i * W),)),
+        (b_left, 1, 1, lambda b, h, i: (cut(b, h, gd_o, t0, 0, tail // 2),)),
         (b_pairs, full, 2, lambda b, h, i: (cut(b, h, gd_o, i * W, 0),)),
         (b_pairs + 1, full, 2, lambda b, h, i: (cut(b, h, gg_o, 0, i * W),)),
         (b_up, full, 1, lambda b, h, i: (cut(b, h, gu_o, 0, i * W),)),
@@ -459,15 +460,6 @@
 
     NB = 512
 
-    def acc_cols(left, w_ref, k, first):
-        for n in range(width // NB):
-            cols = slice(n * NB, (n + 1) * NB)
-            res = jnp.dot(left, w_ref[0:k, cols], preferred_element_type=F32)
-            if first:
-                acc[:, cols] = res
-            else:
-                acc[:, cols] += res
-
     def acc_rows(grad, w_ref):
         for n in range(width // NB):
             cols = slice(n * NB, (n + 1) * NB)
@@ -530,98 +522,16 @@
             def _():
                 total = up32(zs[1, r, :]) + up32(zm[1, r, :])
                 normed, inv = norm_rows(r)
-                back = norm_back(total, normed, inv, gain_ref[...].astype(F32))
+                back = norm_back(total, normed, inv, gain_ref[...])
                 ze[1, r, :] = (up32(cot[r, :]) + back).astype(BF)
                 co(1, p, gin_o).start()
                 cl(1, p, gin_o).start()
 
-    ctx_ld.wait()
-    for cp in cs_ld:
-        cp.wait()
-    for j in range(n_out):
-        left = ctx[:, j * W : (j + 1) * W]
-        w_out(j).wait()
-        acc_cols(left, w_d, W, j == 0)
-        if j + 1 < n_out:
-            w_out(j + 1).start()
-        else:
-            w_down(0).start()
-        put_cols(jnp.int32(j), left.T)
-    hid_ld.wait()
-    for q in range(4):
-        for s in range(2):
-            lo = (2 * q + s) * W
-            hid_t[q, s] = hid[:, lo : lo + W].T
-
     def act_of(g, u):
         return (g * jax.nn.sigmoid(g) * u).astype(BF)
 
     def joined_grad(j):
         return jnp.concatenate([gj[2 * j], gj[2 * j + 1]], axis=1)
-
-    gj_ld.wait()
-
-    def fwd(i, keep):
-        w_gate(i).wait()
-        g = jnp.dot(hid[...], w_a[...], preferred_element_type=F32)
-        w_up(i).wait()
-        u = jnp.dot(hid[...], w_b[...], preferred_element_type=F32)
-
-        @pl.when(i + 1 < full)
-        def _():
-            w_gate(i + 1).start()
-            w_up(i + 1).start()
-
-        @pl.when(i + 1 == full)
-        def _():
-            w_gate_t.start()
-            w_up_t.start()
-
-        gu[i, 0] = g.astype(BF)
-        gu[i, 1] = u.astype(BF)
-        mixed = act_of(g, u)
-
-        @pl.when(i == 0)
-        def _():
-            for b in range(n_out):
-                ev1(jnp.int32(b))
-
-        @pl.when((i >= 2) & (lax.rem(i, 2) == 0))
-        def _():
-            ev1(n_out + i // 2 - 1)
-            ev2(i // 2 - 1)
-
-        w_down(i).wait()
-        acc_cols(mixed, w_d, W, False)
-
-        @pl.when(i + 1 < full)
-        def _():
-            w_down(i + 1).start()
-
-        @pl.when(i + 1 == full)
-        def _():
-            w_down_t.start()
-
-        @pl.when(lax.rem(i, 2) == 1)
-        def _():
-            put_rows(n_out + i // 2, joined_grad(i // 2))
-
-        return keep
-
-    lax.fori_loop(0, full, fwd, 0)
-    w_gate_t.wait()
-    w_up_t.wait()
-    w_qkv(1, 1).start()
-    both = jnp.dot(hid[...], w_a[...], preferred_element_type=F32)
-    w_qkv(0, 0).start()
-    gu[full, 0] = both.astype(BF)
-    mixed = act_of(both[:, 0:tail], both[:, tail:])
-    w_down_t.wait()
-    acc_cols(mixed, w_d, tail, False)
-    w_down(0).start()
-
-    tok_ld.wait()
-    cot_ld.wait()
 
     def cv(k, dev):
         return rdma(svb.at[k], svr.at[k], v_send.at[k], v_recv.at[k], dev)
@@ -665,7 +575,10 @@
     def small_5():
         for k, dev in enumerate(square):
             cw(k, dev).wait_recv()
-        sv_o[...] = (svq[0, 0] + svq[0, 1]) + (svq[1, 0] + svq[1, 1])
+        total = (svq[0, 0] + svq[0, 1]) + (svq[1, 0] + svq[1, 1])
+        for row, ref in enumerate((sg_o, ss_o, sb_o)):
+            for n in range(ref.shape[0]):
+                ref[n : n + 1, :] = total[row : row + 1, n * 128 : (n + 1) * 128]
 
     def small_sent():
         @pl.when(is_end)
@@ -681,34 +594,43 @@
         for k, dev in enumerate(square):
             cw(k, dev).wait_send()
 
-    def to_line(a):
-        def step(p, keep):
-            r = z_rows(p)
-            v = acc[r, :]
-            zs[a, r, :] = v.astype(BF)
-            if a == 0:
-                acc[r, :] = jnp.zeros_like(v)
-            else:
-                normed, _inv = norm_rows(r)
-                svb[0, 0:1, :] += jnp.sum(v * normed, 0, keepdims=True)
-                svb[0, 1:2, :] += jnp.sum(v, 0, keepdims=True)
-
-            return keep
-
+    def send_line(a):
         def send(p, keep):
             ce(a, p).start()
             return keep
 
-        lax.fori_loop(0, n_piece, step, 0)
-
         @pl.when(is_end)
         def _():
             if a == 1:
                 cv(0, mid_dev).start()
             lax.fori_loop(0, n_piece, send, 0)
 
-    to_line(0)
-    put_cols(jnp.int32(b_tail_down), mixed.T)
+    def line_rows(p, keep):
+        r = z_rows(p)
+        v = acc[r, :]
+        zs[1, r, :] = v.astype(BF)
+        normed, _inv = norm_rows(r)
+        svb[0, 0:1, :] += jnp.sum(v * normed, 0, keepdims=True)
+        svb[0, 1:2, :] += jnp.sum(v, 0, keepdims=True)
+        return keep
+
+    z_ld.wait()
+    send_line(0)
+    ctx_ld.wait()
+    for cp in cs_ld:
+        cp.wait()
+    for j in range(n_out):
+        put_cols(jnp.int32(j), ctx[:, j * W : (j + 1) * W].T)
+    hid_ld.wait()
+    for q in range(4):
+        for s in range(2):
+            lo = (2 * q + s) * W
+            hid_t[q, s] = hid[:, lo : lo + W].T
+    for b in range(n_out):
+        ev1(jnp.int32(b))
+    gj_ld.wait()
+    tok_ld.wait()
+    cot_ld.wait()
 
     def joined(n, keep):
         for side in range(2):
@@ -724,17 +646,18 @@
             def _(side=side):
                 (w_gate, w_up)[side](0).start()
 
-            @pl.when(j + early < n_qkv)
-            def _(j=j):
-                b = b_tail_down + 1 + j
-                put_rows(b, joined_grad(j + early))
+            b = n_out + j
+            put_rows(b, joined_grad(j))
+
+            @pl.when(j >= 1)
+            def _(b=b):
                 ev1(b - 1)
 
         ev_e(n)
 
-        @pl.when(n == 1)
-        def _():
-            ev2(jnp.int32(early))
+        @pl.when(n >= 1)
+        def _():
+            ev2(n - 1)
 
         @pl.when(n >= 2)
         def _():
@@ -743,6 +666,7 @@
         return keep
 
     lax.fori_loop(0, n_qkv // 2, joined, 0)
+    gu_ld.wait()
 
     def gate_grads(gm, g, u):
         sg = jax.nn.sigmoid(g)
@@ -754,6 +678,7 @@
         return lax.dot_general(left, w_ref[0:k, :], (((1,), (1,)), ((), ())), preferred_element_type=F32)
 
     e0 = n_qkv // 2
+    two = n_qkv // 2 - 1
 
     def bwd(i, keep):
         w_down(i).wait()
@@ -791,12 +716,11 @@
         e = e0 + 2 * i
         put_cols(b, mixed.T)
         ev1(b - 1)
-        ev2(early + 1 + 2 * i)
         ev_e(e)
         ev_m(e - 2)
         put_rows(b + 1, gu[i, 0])
         ev1(b)
-        ev2(early + 2 + 2 * i)
+        ev2(two + i)
         ev_e(e + 1)
         ev_m(e - 1)
         return keep
@@ -805,6 +729,7 @@
     w_down_t.wait()
     gm = cols_t(cot[...], w_d, tail)
     both = up32(gu[full, 0])
+    mixed = act_of(both[:, 0:tail], both[:, tail:])
     g_gate, g_up = gate_grads(gm, both[:, 0:tail], both[:, tail:])
     both = jnp.concatenate([g_gate, g_up], axis=1)
     gu[full, 0] = both
@@ -813,37 +738,36 @@
     acc_rows(both, w_a)
     svb[0] = jnp.zeros_like(svb[0])
     svb[0, 2:3, 0 : n_qkv * W] = bias_ref[...]
-    to_line(1)
-
+    lax.fori_loop(0, n_piece, line_rows, 0)
+    send_line(1)
+
+    put_cols(jnp.int32(b_left), mixed.T)
+    ev1(jnp.int32(b_left - 1))
     e0 = e0 + 2 * full
+    two = two + full
+    ev2(jnp.int32(two))
+    ev_e(jnp.int32(e0))
+    ev_m(jnp.int32(e0 - 2))
 
     def left_over(i, keep):
         b = b_up + i
         at = jnp.where(i == full, 0, 1)
         put_rows(b, gu[i, at])
         ev1(b - 1)
-
-        @pl.when(lax.rem(i, 2) == 0)
-        def _():
-            ev2(early + 1 + 2 * full + i // 2)
-            ev_e(e0 + i // 2)
-            ev_m(e0 + i // 2 - 2)
-
+        ev2(two + 1 + i)
+        ev_e(e0 + 1 + i)
+        ev_m(e0 - 1 + i)
         return keep
 
     lax.fori_loop(0, full + 1, left_over, 0)
     ev1(jnp.int32(n_batch - 1))
-    e0 = e0 + (full + 2) // 2
+    e0 = e0 + full + 2
+    two_left = two + full + 2
 
     n_e = 2 * n_piece
-    two = early + 1 + 2 * full + (full + 2) // 2
     smalls = (small_1, small_2, small_3, small_4)
 
     def drain(k, keep):
-        @pl.when(k + two < n_batch)
-        def _():
-            ev2(k + two)
-
         @pl.when(k + e0 < n_e)
         def _():
             ev_e(k + e0)
@@ -851,6 +775,10 @@
         @pl.when(k + e0 - 2 < n_e)
         def _():
             ev_m(k + e0 - 2)
+
+        @pl.when((k >= WAIT2) & (k - WAIT2 + two_left < n_batch))
+        def _():
+            ev2(k - WAIT2 + two_left)
 
         for i, small in enumerate(smalls):
             pl.when(k == SMALL_AT + i)(small)
@@ -864,7 +792,8 @@
 
         return keep
 
-    lax.fori_loop(0, max(LATE + (n_batch + 1) // 2, n_e - e0 + 2), drain, 0)
+    steps = max(LATE + (n_batch + 1) // 2, n_e - e0 + 2, WAIT2 + n_batch - two_left)
+    lax.fori_loop(0, steps, drain, 0)
     small_5()
 
     small_sent()
@@ -902,7 +831,7 @@
     lax.fori_loop(0, n_piece, finish_line, 0)
 
 
-def comm_call(hidden, cot, tokens, ctx, gj, gain, bias_sum, qkv_w, out_w, gate_w, up_w, down_w):
+def comm_call(hidden, cot, tokens, ctx, gj, partial, gu, gain, bias_sum, qkv_w, gate_w, up_w, down_w):
     rows, width = hidden.shape
     hd = ctx.shape[1]
     ff = gate_w.shape[1]
@@ -920,15 +849,17 @@
         out_shape=(
             jax.ShapeDtypeStruct((rows, width), BF),
             jax.ShapeDtypeStruct((rows, width), BF),
-            jax.ShapeDtypeStruct((8, width), F32),
+            jax.ShapeDtypeStruct((width // 128, 128), F32),
+            jax.ShapeDtypeStruct((width // 128, 128), F32),
+            jax.ShapeDtypeStruct((n_qkv * W // 128, 128), F32),
             jax.ShapeDtypeStruct((W, n_qkv * W), BF),
             jax.ShapeDtypeStruct((hd, W), BF),
             jax.ShapeDtypeStruct((W, ff), BF),
             jax.ShapeDtypeStruct((W, ff), BF),
             jax.ShapeDtypeStruct((ff, W), BF),
         ),
-        in_specs=[any_spec] * 5 + [vm_spec] * 2 + [any_spec] * 5,
-        out_specs=(any_spec, any_spec, vm_spec) + (any_spec,) * 5,
+        in_specs=[any_spec] * 7 + [vm_spec] * 2 + [any_spec] * 4,
+        out_specs=(any_spec,) * 2 + (vm_spec,) * 3 + (any_spec,) * 5,
         scratch_shapes=[
             vm((4, 2, W, rows), BF),
             vm((rows, width), BF),
@@ -952,7 +883,7 @@
             vm((5, 8, width), F32),
             vm((4, 8, width), F32),
             vm((2, 2, 8, width), F32),
-            dma((13,)),
+            dma((15,)),
             dma((3,)),
             dma((4,)),
             dma((n_batch,)),
@@ -975,7 +906,74 @@
             collective_id=0, has_side_effects=True, vmem_limit_bytes=67043328
         ),
         name="ffn_and_sums",
-    )(hidden, cot, tokens, ctx, gj, gain[None, :], bias_sum, qkv_w, out_w, gate_w, up_w, down_w)
+    )(hidden, cot, tokens, ctx, gj, partial, gu, gain, bias_sum, qkv_w, gate_w, up_w, down_w)
+
+
+def forward_kernel(full, tail, hid, ctx, out_w, gate_w, up_w, down_w, z_o, gu_o, acc):
+    i = pl.program_id(0)
+    width = acc.shape[1]
+    blocks = [slice(n, n + 512) for n in range(0, width, 512)]
+
+    def dot(a, b):
+        return jnp.dot(a, b, preferred_element_type=F32)
+
+    def act_of(g, u):
+        return (g * jax.nn.sigmoid(g) * u).astype(BF)
+
+    @pl.when(i == 0)
+    def _():
+        for cols in blocks:
+            acc[:, cols] = dot(ctx[...], out_w[:, cols])
+
+    @pl.when(i < full)
+    def _():
+        g = dot(hid[...], gate_w[...])
+        u = dot(hid[...], up_w[...])
+        gu_o[0, 0] = g.astype(BF)
+        gu_o[0, 1] = u.astype(BF)
+        mixed = act_of(g, u)
+        for cols in blocks:
+            acc[:, cols] += dot(mixed, down_w[:, cols])
+
+    @pl.when(i == full)
+    def _():
+        both = dot(hid[...], jnp.concatenate([gate_w[:, 0:tail], up_w[:, 0:tail]], axis=1))
+        gu_o[0, 0] = both.astype(BF)
+        gu_o[0, 1] = jnp.zeros_like(both).astype(BF)
+        mixed = act_of(both[:, 0:tail], both[:, tail:])
+        for cols in blocks:
+            z_o[:, cols] = (acc[:, cols] + dot(mixed, down_w[0:tail, cols])).astype(BF)
+
+
+def forward_call(hidden, ctx, out_w, gate_w, up_w, down_w):
+    rows, width = hidden.shape
+    hd = ctx.shape[1]
+    ff = gate_w.shape[1]
+    full, tail = ff // W, ff % W
+    once = lambda shape: pl.BlockSpec(shape, lambda i: (0,) * len(shape), pipeline_mode=pl.Buffered(1))
+    return pl.pallas_call(
+        functools.partial(forward_kernel, full, tail),
+        grid=(full + 1,),
+        out_shape=(
+            jax.ShapeDtypeStruct((rows, width), BF),
+            jax.ShapeDtypeStruct((full + 1, 2, rows, W), BF),
+        ),
+        in_specs=[
+            once((rows, width)),
+            once((rows, hd)),
+            once((hd, width)),
+            pl.BlockSpec((width, W), lambda i: (0, i)),
+            pl.BlockSpec((width, W), lambda i: (0, i)),
+            pl.BlockSpec((W, width), lambda i: (i, 0)),
+        ],
+        out_specs=(
+            once((rows, width)),
+            pl.BlockSpec((1, 2, rows, W), lambda i: (i, 0, 0, 0)),
+        ),
+        scratch_shapes=[pltpu.VMEM((rows, width), F32)],
+        compiler_params=pltpu.CompilerParams(vmem_limit_bytes=60 << 20),
+        name="forward",
+    )(hidden, ctx, out_w, gate_w, up_w, down_w)
 
 
 QB = 128
@@ -983,22 +981,30 @@
 
 
 def attn_kernel(
-    heads_scale, tok, seg_ref, gain_ref, shift_ref, freq_ref, w_ref, b_ref, ow_ref, cot,
-    hid, ctx_o, gj_o, bias_o,
-    bias_m, tab, s_m, g_m, p_m, gs_m,
+    heads_scale, tok, seg_ref, gain_ref, shift_ref, b_ref, w_ref, ow_ref, cot,
+    hid, ctx_o, gj_o, bias_o, gain_o,
+    bias_m, tab, s_m, g_m, p_m, gs_m, shift_m, b_m,
 ):
     rows = tok.shape[0]
     nq = rows // QB
     half = ROT // 2
 
-    @pl.when(pl.program_id(0) == 0)
+    step = pl.program_id(0)
+
+    @pl.when(step == 0)
     def _():
+        for n in range(gain_ref.shape[0]):
+            cols = slice(n * QB, (n + 1) * QB)
+            gain_o[0:1, cols] = gain_ref[n : n + 1, :].astype(F32)
+            shift_m[0:1, cols] = shift_ref[n : n + 1, :].astype(F32)
+        b_m[...] = b_ref[...].astype(F32)
+
         def norm_step(n, keep):
             r = pl.ds(pl.multiple_of(n * 64, 64), 64)
             v = tok[r, :].astype(F32)
             v = v - jnp.mean(v, -1, keepdims=True)
             v = v * lax.rsqrt(jnp.mean(v * v, -1, keepdims=True) + EPSILON)
-            hid[r, :] = (v * gain_ref[...].astype(F32) + shift_ref[...].astype(F32)).astype(BF)
+            hid[r, :] = (v * gain_o[...] + shift_m[...]).astype(BF)
             return keep
 
         lax.fori_loop(0, rows // 64, norm_step, 0)
@@ -1006,6 +1012,9 @@
         seg_t = jnp.broadcast_to(seg, (8, rows)).T
         lane = lax.broadcasted_iota(jnp.int32, (QB, QB), 1)
         head_lane = lane % DH
+        freq = jnp.ones((1, QB), F32)
+        for n in range(1, half):
+            freq = jnp.where(head_lane[0:1] % half == n, 10000.0 ** (-2.0 * n / ROT), freq)
         for i in range(nq):
             lo = max(0, i - 2) * QB
             n = (i + 1) * QB - lo
@@ -1015,7 +1024,7 @@
             allowed = same & (q_at >= k_at)
             bias_m[i, :, 0:n] = jnp.where(allowed, 0.0, NEGATIVE)
             place = jnp.sum(jnp.where(allowed, 1.0, 0.0), -1, keepdims=True) - 1.0
-            angle = place * freq_ref[...]
+            angle = place * freq
             cosine, sine = jnp.cos(angle), jnp.sin(angle)
             for blk in range(3):
                 live = head_lane < ROT
@@ -1039,10 +1048,10 @@
     def dot(a, b):
         return jnp.dot(a, b, preferred_element_type=F32)
 
-    joined = dot(hid[...], w_ref[...]) + b_ref[...].astype(F32)
+    joined = dot(hid[...], w_ref[...])
     turned = []
     for blk in range(3):
-        v = joined[:, blk * QB : (blk + 1) * QB]
+        v = joined[:, blk * QB : (blk + 1) * QB] + b_m[pl.ds(3 * step + blk, 1), :]
         v = v * tab[blk, 0] + pltpu.roll(v, QB - half, 1) * tab[blk, 1] + pltpu.roll(v, half, 1) * tab[blk, 2]
         turned.append(v.astype(BF))
     gctx = dot_t(cot[...], ow_ref[...]).astype(BF)
@@ -1103,8 +1112,6 @@
     hd = out_w.shape[0]
     steps = hd // (2 * DH)
     three = 3 * QB
-    lane = jnp.arange(QB) % DH % (ROT // 2)
-    freq = jnp.power(10000.0, -2.0 * lane.astype(F32) / ROT)[None, :]
     whole = lambda shape: pl.BlockSpec(shape, lambda i: (0,) * len(shape))
     once = lambda shape: pl.BlockSpec(shape, lambda i: (0,) * len(shape), pipeline_mode=pl.Buffered(1))
     return pl.pallas_call(
@@ -1115,15 +1122,15 @@
             jax.ShapeDtypeStruct((rows, hd), BF),
             jax.ShapeDtypeStruct((3 * steps, rows, QB), BF),
             jax.ShapeDtypeStruct((1, 3 * hd), F32),
+            jax.ShapeDtypeStruct((1, width), F32),
         ),
         in_specs=[
             once((rows, width)),
             whole((1, rows)),
-            whole((1, width)),
-            whole((1, width)),
-            whole((1, QB)),
+            whole((width // QB, QB)),
+            whole((width // QB, QB)),
+            whole((3 * hd // QB, QB)),
             pl.BlockSpec((width, three), lambda i: (0, i)),
-            pl.BlockSpec((1, three), lambda i: (0, i)),
             pl.BlockSpec((QB, width), lambda i: (i, 0)),
             once((rows, width)),
         ],
@@ -1132,6 +1139,7 @@
             pl.BlockSpec((rows, QB), lambda i: (0, i)),
             pl.BlockSpec((3, rows, QB), lambda i: (i, 0, 0)),
             pl.BlockSpec((1, three), lambda i: (0, i)),
+            whole((1, width)),
         ),
         scratch_shapes=[
             pltpu.VMEM((rows // QB, QB, three), F32),
@@ -1140,10 +1148,14 @@
             pltpu.VMEM((2, rows // QB, QB, three), F32),
             pltpu.VMEM((2, rows // QB, QB, three), BF),
             pltpu.VMEM((2, rows // QB, QB, three), BF),
+            pltpu.VMEM((1, width), F32),
+            pltpu.VMEM((3 * hd // QB, QB), F32),
         ],
         compiler_params=pltpu.CompilerParams(vmem_limit_bytes=60 << 20),
         name="attention",
-    )(tokens, segment_ids, gain[None, :], shift[None, :], freq, qkv_w, qkv_b[None, :], out_w, cot)
+    )(
+        tokens, segment_ids, gain.reshape(-1, QB), shift.reshape(-1, QB), qkv_b.reshape(-1, QB), qkv_w, out_w, cot
+    )
 
 
 def fast(
@@ -1176,21 +1188,22 @@
     )
     if not fits:
         return local(*args)
-    hidden_in, context, grad_joined, bias_local = attn_call(
+    hidden_in, context, grad_joined, bias_local, gain_row = attn_call(
         tokens, segment_ids, norm_gain, norm_bias, qkv_weight, qkv_bias, out_weight, cotangent
     )
-    output, grad_input, small, *sums = comm_call(
-        hidden_in, cotangent, tokens, context, grad_joined, norm_gain, bias_local,
-        qkv_weight, out_weight, gate_weight, up_weight, down_weight,
+    partial, gate_up = forward_call(hidden_in, context, out_weight, gate_weight, up_weight, down_weight)
+    output, grad_input, gain_sum, shift_sum, bias_sum, *sums = comm_call(
+        hidden_in, cotangent, tokens, context, grad_joined, partial, gate_up, gain_row, bias_local,
+        qkv_weight, gate_weight, up_weight, down_weight,
     )
     joined_w, out_w, gate_w, up_w, down_w = (v.astype(F32) for v in sums)
     return (
         output,
         grad_input,
-        small[0],
-        small[1],
+        gain_sum.reshape(width),
+        shift_sum.reshape(width),
         joined_w,
-        small[2, : qkv_weight.shape[1]],
+        bias_sum.reshape(qkv_weight.shape[1]),
         out_w,
         gate_w,
         up_w,

time: 198 us -> 188 us (0.949)
  Pallas kernels: 179 us -> 173 us
  local copies, waits for them, and re-layouts: 10.5 us -> 5.49 us
    pallas_call x1, Pallas kernels: 153 us -> 129 us  [comm_call(): pl.pallas_call(functools.partial(comm_kernel, dims), out_shape=(jax.Shape...]
    pallas_call x0 -> x1, Pallas kernels: none -> 18.1 us  [forward_call(): pl.pallas_call(functools.partial(forward_kernel, full, tail), grid=(full...]
    broadcast_in_dim x3 -> x0, local copies, waits for them, and re-layouts: 3.87 us -> none  [the longest x1 1.29 us: attn_call(): gain[None, :]]
    slice x2 -> x0, local copies, waits for them, and re-layouts: 2.97 us -> none  [the longest x1 1.55 us: fast(): small[1]]
    unnamed x14 -> x21, local copies, waits for them, and re-layouts: 3.68 us -> 5.49 us
where the time goes in v2:
time: 188 us; the launch traced here: 187 us
  Pallas kernels  173 us (92%)
  other arithmetic  7.95 us (4%)
  local copies, waits for them, and re-layouts  5.49 us (3%)
    pallas_call x1, Pallas kernels, comm_call(): pl.pallas_call(functools.partial(comm_kernel, dims), out_shape=(jax.Shape...  129 us
    pallas_call x1, Pallas kernels, attn_call(): pl.pallas_call(functools.partial(attn_kernel, DH ** (-0.5)), grid=(steps,...  25.9 us
    pallas_call x1, Pallas kernels, forward_call(): pl.pallas_call(functools.partial(forward_kernel, full, tail), grid=(full...  18.1 us
    convert_element_type x5, other arithmetic, fast(): joined_w, out_w, gate_w, up_w, down_w = (v.astype(F32) for v in sums)  7.95 us
    unnamed x21, local copies, waits for them, and re-layouts  5.49 us

profile of v2, /device:TPU:0, one launch (start us, length us, event | category | flops | bytes accessed | tf_op | source)
XLA Modules:
  0.0 187.4 jit_solution(13792618774309835311)
XLA Ops:
  0.6 25.9 %attention.1 = (bf16[512,2048]{1,0:T(8,128)(2,1)}, bf16[512,512]{1,0:T(8,128)(2,1)}, bf16[12,512,128]{2,1,0:T(8,128)(2,1)}, f32[1,1536]{1,0:T(1,128)}, f32[1,2048]{1,0:T(1,128)}) custom-call(bf16[512,2048]{1,0:T(8,128)(2,1)} %tok_h.1, s32[1,512]{1,0:T(1,128)} %seg_ref.1, bf16[16,128]{1,0:T(8,128)(2,1)} %bitcast.9, bf16[16,128]{1,0:T(8,128)(2,1)} %bitcast.10, ...), custom_call_target="tpu_custom_call" | custom-call | tf_op jit(solution)/shard_map/attention/pallas_call | solution.py:1117
  26.5 18.1 %forward.1 = (bf16[512,2048]{1,0:T(8,128)(2,1)}, bf16[6,2,512,256]{3,2,1,0:T(8,128)(2,1)}) custom-call(bf16[512,2048]{1,0:T(8,128)(2,1)} %get-tuple-element.27.hid.hid_h, bf16[512,512]{1,0:T(8,128)(2,1)} %get-tuple-element.28.ctx.ctx_h, bf16[512,2048]{1,0:T(8,128)(2,1)} %out_w.1, bf16[2048,1408]{1,0:T(8,128)(2,1)} %gate_h.1, bf16[2048,1408]{1,0:T(8,128)(2,1)} %up_h.1, ...), custom_call_target="tpu_custom_call" | custom-call | tf_op jit(solution)/shard_map/forward/pallas_call | solution.py:954
  44.6 129.3 %ffn_and_sums.1 = (bf16[512,2048]{1,0:T(8,128)(2,1)}, bf16[512,2048]{1,0:T(8,128)(2,1)}, f32[16,128]{1,0:T(8,128)}, f32[16,128]{1,0:T(8,128)}, f32[12,128]{1,0:T...) custom-call(bf16[512,2048]{1,0:T(8,128)(2,1)} %get-tuple-element.27., ...), custom_call_target="tpu_custom_call" | custom-call | tf_op jit(solution)/shard_map/ffn_and_sums/pallas_call | solution.py:847
  174.0 0.0 copy-start.4
  174.0 1.8 convert_element_type.16
  175.8 0.0 copy-start.3
  175.8 2.4 %convert_element_type.17 = f32[256,1408]{1,0:T(8,128)} convert(bf16[256,1408]{1,0:T(8,128)(2,1)} %get-tuple-element.41) | non-fusion elementwise | flops 360448 | bytes 2162688 | tf_op jit(solution)/shard_map/convert_element_type | solution.py:1199
  178.2 0.0 copy-done.4
  178.2 0.0 copy-start.2
  178.2 1.2 convert_element_type.18
  179.4 0.0 copy-done.3
  179.4 0.0 copy-start.1
  179.4 1.2 convert_element_type.19
  180.6 0.0 copy-done.2
  180.6 1.3 convert_element_type.15
  181.9 0.0 copy-done.1
  181.9 0.0 copy-start
  181.9 1.3 copy.26
  183.3 1.0 copy-done
  184.3 0.0 copy-start.7
  184.3 0.0 copy-start.6
  184.3 0.0 copy-start.5
  184.3 1.3 copy.27
  185.6 0.0 copy-done.7
  185.6 0.6 copy.28
  186.2 0.0 copy-done.6
  186.2 0.6 copy.29
  186.8 0.0 copy-done.5
  186.8 0.6 copy.30
Async XLA Ops:
  174.0 4.2 %copy-start.4 = (bf16[256,1408]{1,0:T(8,128)(2,1)S(1)}, bf16[256,1408]{1,0:T(8,128)(2,1)}, u32[]{:S(2)}) copy-start(bf16[256,1408]{1,0:T(8,128)(2,1)} %get-tuple-element.42) | copy-start | bytes 2162692
  175.8 3.6 %copy-start.3 = (bf16[1408,256]{1,0:T(8,128)(2,1)S(1)}, bf16[1408,256]{1,0:T(8,128)(2,1)}, u32[]{:S(2)}) copy-start(bf16[1408,256]{1,0:T(8,128)(2,1)} %get-tuple-element.43) | copy-start | bytes 2162692
  178.2 2.4 %copy-start.2 = (bf16[256,1536]{1,0:T(8,128)(2,1)S(1)}, bf16[256,1536]{1,0:T(8,128)(2,1)}, u32[]{:S(2)}) copy-start(bf16[256,1536]{1,0:T(8,128)(2,1)} %get-tuple-element.38) | copy-start | bytes 2359300
  179.4 2.5 %copy-start.1 = (bf16[512,2048]{1,0:T(8,128)(2,1)S(1)}, bf16[512,2048]{1,0:T(8,128)(2,1)}, u32[]{:S(2)}) copy-start(bf16[512,2048]{1,0:T(8,128)(2,1)} %get-tuple-element.54) | copy-start | bytes 6291460
  181.9 2.3 %copy-start = (bf16[512,2048]{1,0:T(8,128)(2,1)S(1)}, bf16[512,2048]{1,0:T(8,128)(2,1)}, u32[]{:S(2)}) copy-start(bf16[512,2048]{1,0:T(8,128)(2,1)} %get-tuple-element.55) | copy-start | bytes 6291460
  184.3 1.3 copy-start.7
  184.3 1.9 %copy-start.6 = (f32[16,128]{1,0:T(8,128)S(1)}, f32[16,128]{1,0:T(8,128)}, u32[]{:S(2)}) copy-start(f32[16,128]{1,0:T(8,128)} %get-tuple-element.37) | copy-start | bytes 24580
  184.3 2.5 %copy-start.5 = (f32[12,128]{1,0:T(8,128)S(1)}, f32[12,128]{1,0:T(8,128)}, u32[]{:S(2)}) copy-start(f32[12,128]{1,0:T(8,128)} %get-tuple-element.39) | copy-start | bytes 18436

commit v3 on v2

--- a/solution.py
+++ b/solution.py
@@ -976,6 +976,32 @@
     )(hidden, ctx, out_w, gate_w, up_w, down_w)
 
 
+PARTS = 4
+
+
+def finish_kernel(*refs):
+    n = len(refs) // 2
+    for src, dst in zip(refs[:n], refs[n:]):
+        dst[...] = src[...].astype(dst.dtype)
+
+
+def finish_call(values, types):
+    def spec(v):
+        if v.shape[0] < 16 * PARTS:
+            return pl.BlockSpec(v.shape, lambda i: (0, 0))
+        return pl.BlockSpec((v.shape[0] // PARTS, v.shape[1]), lambda i: (i, 0))
+
+    return pl.pallas_call(
+        finish_kernel,
+        grid=(PARTS,),
+        out_shape=tuple(jax.ShapeDtypeStruct(v.shape, t) for v, t in zip(values, types)),
+        in_specs=[spec(v) for v in values],
+        out_specs=tuple(spec(v) for v in values),
+        compiler_params=pltpu.CompilerParams(vmem_limit_bytes=60 << 20),
+        name="finish",
+    )(*values)
+
+
 QB = 128
 ROWS = 32
 
@@ -1192,11 +1218,13 @@
         tokens, segment_ids, norm_gain, norm_bias, qkv_weight, qkv_bias, out_weight, cotangent
     )
     partial, gate_up = forward_call(hidden_in, context, out_weight, gate_weight, up_weight, down_weight)
-    output, grad_input, gain_sum, shift_sum, bias_sum, *sums = comm_call(
+    results = comm_call(
         hidden_in, cotangent, tokens, context, grad_joined, partial, gate_up, gain_row, bias_local,
         qkv_weight, gate_weight, up_weight, down_weight,
     )
-    joined_w, out_w, gate_w, up_w, down_w = (v.astype(F32) for v in sums)
+    output, grad_input, gain_sum, shift_sum, bias_sum, joined_w, out_w, gate_w, up_w, down_w = finish_call(
+        results, (BF,) * 2 + (F32,) * 8
+    )
     return (
         output,
         grad_input,

time: 188 us -> 182 us (0.968)
  Pallas kernels: 173 us -> 181 us
  other arithmetic: 7.95 us -> 0 us
  local copies, waits for them, and re-layouts: 5.49 us -> 0 us
    convert_element_type x5 -> x0, other arithmetic: 7.95 us -> none  [fast(): joined_w, out_w, gate_w, up_w, down_w = (v.astype(F32) for v in sums)]
    pallas_call x0 -> x1, Pallas kernels: none -> 7.23 us  [finish_call(): pl.pallas_call(finish_kernel, grid=(PARTS,), out_shape=tuple((jax.ShapeDt...]
    unnamed x21 -> x0, local copies, waits for them, and re-layouts: 5.49 us -> none
where the time goes in v3:
time: 182 us; the launch traced here: 181 us
  Pallas kernels  181 us (99%)
    pallas_call x1, Pallas kernels, comm_call(): pl.pallas_call(functools.partial(comm_kernel, dims), out_shape=(jax.Shape...  129 us
    pallas_call x1, Pallas kernels, attn_call(): pl.pallas_call(functools.partial(attn_kernel, DH ** (-0.5)), grid=(steps,...  25.9 us
    pallas_call x1, Pallas kernels, forward_call(): pl.pallas_call(functools.partial(forward_kernel, full, tail), grid=(full...  18.1 us
    pallas_call x1, Pallas kernels, finish_call(): pl.pallas_call(finish_kernel, grid=(PARTS,), out_shape=tuple((jax.ShapeDt...  7.23 us

profile of v3, /device:TPU:0, one launch (start us, length us, event | category | flops | bytes accessed | tf_op | source)
XLA Modules:
  0.0 181.4 jit_solution(1441688425694563953)
XLA Ops:
  0.6 25.9 %attention.1 = (bf16[512,2048]{1,0:T(8,128)(2,1)}, bf16[512,512]{1,0:T(8,128)(2,1)}, bf16[12,512,128]{2,1,0:T(8,128)(2,1)}, f32[1,1536]{1,0:T(1,128)}, f32[1,2048]{1,0:T(1,128)}) custom-call(bf16[512,2048]{1,0:T(8,128)(2,1)} %tok_h.1, s32[1,512]{1,0:T(1,128)} %seg_ref.1, bf16[16,128]{1,0:T(8,128)(2,1)} %bitcast.6, bf16[16,128]{1,0:T(8,128)(2,1)} %bitcast.7, ...), custom_call_target="tpu_custom_call" | custom-call | tf_op jit(solution)/shard_map/attention/pallas_call | solution.py:1143
  26.5 18.1 %forward.1 = (bf16[512,2048]{1,0:T(8,128)(2,1)}, bf16[6,2,512,256]{3,2,1,0:T(8,128)(2,1)}) custom-call(bf16[512,2048]{1,0:T(8,128)(2,1)} %get-tuple-element.37.hid.hid_h, bf16[512,512]{1,0:T(8,128)(2,1)} %get-tuple-element.38.ctx.ctx_h, bf16[512,2048]{1,0:T(8,128)(2,1)} %out_w.1, bf16[2048,1408]{1,0:T(8,128)(2,1)} %gate_h.1, bf16[2048,1408]{1,0:T(8,128)(2,1)} %up_h.1, ...), custom_call_target="tpu_custom_call" | custom-call | tf_op jit(solution)/shard_map/forward/pallas_call | solution.py:954
  44.6 129.3 %ffn_and_sums.1 = (bf16[512,2048]{1,0:T(8,128)(2,1)}, bf16[512,2048]{1,0:T(8,128)(2,1)}, f32[16,128]{1,0:T(8,128)}, f32[16,128]{1,0:T(8,128)}, f32[12,128]{1,0:T...) custom-call(bf16[512,2048]{1,0:T(8,128)(2,1)} %get-tuple-element.37., ...), custom_call_target="tpu_custom_call" | custom-call | tf_op jit(solution)/shard_map/ffn_and_sums/pallas_call | solution.py:847
  174.0 7.2 %finish.1 = (bf16[512,2048]{1,0:T(8,128)(2,1)}, bf16[512,2048]{1,0:T(8,128)(2,1)}, f32[16,128]{1,0:T(8,128)}, f32[16,128]{1,0:T(8,128)}, f32[12,128]{1,0:T(8,128...) custom-call(bf16[512,2048]{1,0:T(8,128)(2,1)} %get-tuple-element.44., ...), custom_call_target="tpu_custom_call" | custom-call | tf_op jit(solution)/shard_map/finish/pallas_call | solution.py:994

commit v4 on v3

--- a/solution.py
+++ b/solution.py
@@ -1041,6 +1041,8 @@
         freq = jnp.ones((1, QB), F32)
         for n in range(1, half):
             freq = jnp.where(head_lane[0:1] % half == n, 10000.0 ** (-2.0 * n / ROT), freq)
+        group = QB // nq
+        packed = jnp.zeros((QB, QB), F32)
         for i in range(nq):
             lo = max(0, i - 2) * QB
             n = (i + 1) * QB - lo
@@ -1050,8 +1052,18 @@
             allowed = same & (q_at >= k_at)
             bias_m[i, :, 0:n] = jnp.where(allowed, 0.0, NEGATIVE)
             place = jnp.sum(jnp.where(allowed, 1.0, 0.0), -1, keepdims=True) - 1.0
-            angle = place * freq
-            cosine, sine = jnp.cos(angle), jnp.sin(angle)
+            packed = jnp.where(lane // group == i, place, packed)
+        angle = packed * freq
+        tables = jnp.cos(angle), jnp.sin(angle)
+        for i in range(nq):
+            cosine, sine = (
+                jnp.where(
+                    lane < DH,
+                    pltpu.roll(t, (QB - group * i) % QB, 1) if i else t,
+                    pltpu.roll(t, (QB + DH - group * i) % QB, 1) if DH != group * i else t,
+                )
+                for t in tables
+            )
             for blk in range(3):
                 live = head_lane < ROT
                 if blk == 1:
@@ -1211,6 +1223,7 @@
         and out_weight.shape[0] % W == 0
         and qkv_weight.shape[1] == 3 * out_weight.shape[0]
         and 2 * DH == QB
+        and 4 * ROT <= QB
     )
     if not fits:
         return local(*args)

time: 182 us -> 181 us (level)
  no operation moved by 1% of the time
where the time goes in v4:
time: 181 us
  Pallas kernels  180 us (99%)
    pallas_call x1, Pallas kernels, comm_call(): pl.pallas_call(functools.partial(comm_kernel, dims), out_shape=(jax.Shape...  129 us
    pallas_call x1, Pallas kernels, attn_call(): pl.pallas_call(functools.partial(attn_kernel, DH ** (-0.5)), grid=(steps,...  25.5 us
    pallas_call x1, Pallas kernels, forward_call(): pl.pallas_call(functools.partial(forward_kernel, full, tail), grid=(full...  18.1 us
    pallas_call x1, Pallas kernels, finish_call(): pl.pallas_call(finish_kernel, grid=(PARTS,), out_shape=tuple((jax.ShapeDt...  7.23 us

profile of v4, /device:TPU:0, one launch (start us, length us, event | category | flops | bytes accessed | tf_op | source)
XLA Modules:
  0.0 181.0 jit_solution(2658227599737257922)
XLA Ops:
  0.6 25.5 %attention.1 = (bf16[512,2048]{1,0:T(8,128)(2,1)}, bf16[512,512]{1,0:T(8,128)(2,1)}, bf16[12,512,128]{2,1,0:T(8,128)(2,1)}, f32[1,1536]{1,0:T(1,128)}, f32[1,2048]{1,0:T(1,128)}) custom-call(bf16[512,2048]{1,0:T(8,128)(2,1)} %tok_h.1, s32[1,512]{1,0:T(1,128)} %seg_ref.1, bf16[16,128]{1,0:T(8,128)(2,1)} %bitcast.6, bf16[16,128]{1,0:T(8,128)(2,1)} %bitcast.7, ...), custom_call_target="tpu_custom_call" | custom-call | tf_op jit(solution)/shard_map/attention/pallas_call | solution.py:1155
  26.1 18.1 %forward.1 = (bf16[512,2048]{1,0:T(8,128)(2,1)}, bf16[6,2,512,256]{3,2,1,0:T(8,128)(2,1)}) custom-call(bf16[512,2048]{1,0:T(8,128)(2,1)} %get-tuple-element.37.hid.hid_h, bf16[512,512]{1,0:T(8,128)(2,1)} %get-tuple-element.38.ctx.ctx_h, bf16[512,2048]{1,0:T(8,128)(2,1)} %out_w.1, bf16[2048,1408]{1,0:T(8,128)(2,1)} %gate_h.1, bf16[2048,1408]{1,0:T(8,128)(2,1)} %up_h.1, ...), custom_call_target="tpu_custom_call" | custom-call | tf_op jit(solution)/shard_map/forward/pallas_call | solution.py:954
  44.3 129.3 %ffn_and_sums.1 = (bf16[512,2048]{1,0:T(8,128)(2,1)}, bf16[512,2048]{1,0:T(8,128)(2,1)}, f32[16,128]{1,0:T(8,128)}, f32[16,128]{1,0:T(8,128)}, f32[12,128]{1,0:T...) custom-call(bf16[512,2048]{1,0:T(8,128)(2,1)} %get-tuple-element.37., ...), custom_call_target="tpu_custom_call" | custom-call | tf_op jit(solution)/shard_map/ffn_and_sums/pallas_call | solution.py:847
  173.6 7.2 %finish.1 = (bf16[512,2048]{1,0:T(8,128)(2,1)}, bf16[512,2048]{1,0:T(8,128)(2,1)}, f32[16,128]{1,0:T(8,128)}, f32[16,128]{1,0:T(8,128)}, f32[12,128]{1,0:T(8,128...) custom-call(bf16[512,2048]{1,0:T(8,128)(2,1)} %get-tuple-element.44., ...), custom_call_target="tpu_custom_call" | custom-call | tf_op jit(solution)/shard_map/finish/pallas_call | solution.py:994

commit v5 on v4

--- a/solution.py
+++ b/solution.py
@@ -252,7 +252,7 @@
 PR = 32
 SMALL_AT = 2
 LATE = 8
-WAIT2 = 2
+WAIT2 = 4
 
 
 def comm_kernel(

time: 181 us -> 181 us (level)
  no operation moved by 1% of the time
where the time goes in v5:
time: 181 us
  Pallas kernels  180 us (99%)
    pallas_call x1, Pallas kernels, comm_call(): pl.pallas_call(functools.partial(comm_kernel, dims), out_shape=(jax.Shape...  129 us
    pallas_call x1, Pallas kernels, attn_call(): pl.pallas_call(functools.partial(attn_kernel, DH ** (-0.5)), grid=(steps,...  25.5 us
    pallas_call x1, Pallas kernels, forward_call(): pl.pallas_call(functools.partial(forward_kernel, full, tail), grid=(full...  18.1 us
    pallas_call x1, Pallas kernels, finish_call(): pl.pallas_call(finish_kernel, grid=(PARTS,), out_shape=tuple((jax.ShapeDt...  7.23 us

profile of v5, /device:TPU:0, one launch (start us, length us, event | category | flops | bytes accessed | tf_op | source)
XLA Modules:
  0.0 181.0 jit_solution(10211776191202872879)
XLA Ops:
  0.6 25.5 %attention.1 = (bf16[512,2048]{1,0:T(8,128)(2,1)}, bf16[512,512]{1,0:T(8,128)(2,1)}, bf16[12,512,128]{2,1,0:T(8,128)(2,1)}, f32[1,1536]{1,0:T(1,128)}, f32[1,2048]{1,0:T(1,128)}) custom-call(bf16[512,2048]{1,0:T(8,128)(2,1)} %tok_h.1, s32[1,512]{1,0:T(1,128)} %seg_ref.1, bf16[16,128]{1,0:T(8,128)(2,1)} %bitcast.6, bf16[16,128]{1,0:T(8,128)(2,1)} %bitcast.7, ...), custom_call_target="tpu_custom_call" | custom-call | tf_op jit(solution)/shard_map/attention/pallas_call | solution.py:1155
  26.1 18.1 %forward.1 = (bf16[512,2048]{1,0:T(8,128)(2,1)}, bf16[6,2,512,256]{3,2,1,0:T(8,128)(2,1)}) custom-call(bf16[512,2048]{1,0:T(8,128)(2,1)} %get-tuple-element.37.hid.hid_h, bf16[512,512]{1,0:T(8,128)(2,1)} %get-tuple-element.38.ctx.ctx_h, bf16[512,2048]{1,0:T(8,128)(2,1)} %out_w.1, bf16[2048,1408]{1,0:T(8,128)(2,1)} %gate_h.1, bf16[2048,1408]{1,0:T(8,128)(2,1)} %up_h.1, ...), custom_call_target="tpu_custom_call" | custom-call | tf_op jit(solution)/shard_map/forward/pallas_call | solution.py:954
  44.3 129.3 %ffn_and_sums.1 = (bf16[512,2048]{1,0:T(8,128)(2,1)}, bf16[512,2048]{1,0:T(8,128)(2,1)}, f32[16,128]{1,0:T(8,128)}, f32[16,128]{1,0:T(8,128)}, f32[12,128]{1,0:T...) custom-call(bf16[512,2048]{1,0:T(8,128)(2,1)} %get-tuple-element.37., ...), custom_call_target="tpu_custom_call" | custom-call | tf_op jit(solution)/shard_map/ffn_and_sums/pallas_call | solution.py:847
  173.6 7.2 %finish.1 = (bf16[512,2048]{1,0:T(8,128)(2,1)}, bf16[512,2048]{1,0:T(8,128)(2,1)}, f32[16,128]{1,0:T(8,128)}, f32[16,128]{1,0:T(8,128)}, f32[12,128]{1,0:T(8,128...) custom-call(bf16[512,2048]{1,0:T(8,128)(2,1)} %get-tuple-element.44., ...), custom_call_target="tpu_custom_call" | custom-call | tf_op jit(solution)/shard_map/finish/pallas_call | solution.py:994
